TPU v7x, 256 devices: a whole 4x4x8 slice. The times are simulated.
256 devices in a mesh: section: 8 (over z_hi, core), fsdp: 4 (over x), tensor: 8 (over y, z_lo).
Axes of the slice: x: 4, y: 4, z: 8 (z_hi: 4, z_lo: 2; z = z_hi * 2 + z_lo), core: 2. Of those that a mesh axis runs over, the one named last changes fastest.
Arguments:
- hidden: bfloat16 [8, 512, 8192], P('section', 'fsdp', 'tensor'), may hold values from -16 to 16
- encoder_weight: bfloat16 [8, 1024, 8192], P('section', 'fsdp', 'tensor'), may hold values from -0.0625 to 0.0625
- decoder_weight: bfloat16 [8, 1024, 8192], P('section', 'fsdp', 'tensor'), may hold values from -16 to 16
- query_weight: bfloat16 [8, 8192, 8192], P('section', 'fsdp', 'tensor'), may hold values from -32 to 32
- key_weight: bfloat16 [8, 8192, 1024], P('section', 'fsdp', 'tensor'), may hold values from -1 to 1
- value_weight: bfloat16 [8, 8192, 1024], P('section', 'fsdp', 'tensor'), may hold values from -0.0625 to 0.0625
- segments: int32 [8, 4, 128], P('section', 'fsdp'), may hold values from 0 to 3, never falling along the last dimension, each value on 1 to 64 neighbouring positions
- out_grad: bfloat16 [8, 512, 8192], P('section', 'fsdp', 'tensor'), may hold values from -6 to 6
Outputs:
- attention: bfloat16 [8, 512, 8192], P('section', 'fsdp', 'tensor')
- hidden_grad: bfloat16 [8, 512, 8192], P('section', 'fsdp', 'tensor')
- encoder_grad: float32 [8, 1024, 8192], P('section', 'fsdp', 'tensor')
- decoder_grad: float32 [8, 1024, 8192], P('section', 'fsdp', 'tensor')
Inputs may be any that keep to these rules, and one draw needn't show every extreme that they name: `segments`: segment ids never fall along a row, and attention stays inside one document of one row; each document spans at most 64 tokens, and some document spans exactly that many.
All inputs are finite; a program needn't handle non-finite values.
Results may differ from a plain program's by a relative error of at most 0.025.
Values may be sent and summed in bfloat16 or wider, within the bound.
No kernel may reach another device: no remote copies, remote signals or barrier semaphores. Data moves between devices by JAX's collectives and lax.ppermute only.
A program may use at most 128 MiB of HBM per device.

v0:
```python
import math

import jax
import jax.numpy as jnp
from jax import lax
from jax.sharding import PartitionSpec as P

D = 8192
DH = 128


NORM_EPS = 1e-05
ROPE_BASE = 500000.0
NEG_FILL = -1e30


def passed_along(value, axis, steps):
    count = lax.axis_size(axis)
    pairs = [(source, (source + steps) % count) for source in range(count)]
    return lax.ppermute(value, axis, pairs)


def rope_tables(segment_row, dim):
    length = segment_row.shape[0]
    positions = jnp.arange(length, dtype=jnp.int32)
    earlier = jnp.sum((segment_row[None, :] < segment_row[:, None]).astype(jnp.int32), axis=1)
    places = (positions - earlier).astype(jnp.float32)
    frequency = jnp.exp(jnp.arange(0, dim, 2).astype(jnp.float32) * (-math.log(ROPE_BASE) / dim))
    angles = places[:, None] * frequency[None, :]
    allowed = (segment_row[None, :] == segment_row[:, None]) & (
        positions[None, :] <= positions[:, None]
    )
    return (jnp.cos(angles), jnp.sin(angles), allowed)


def rotate(values, cosine, sine):
    half_dim = values.shape[-1] // 2
    first_half = values[..., :half_dim]
    second_half = values[..., half_dim:]
    cosine_rows = cosine[:, None, :]
    sine_rows = sine[:, None, :]
    return jnp.concatenate(
        [
            first_half * cosine_rows - second_half * sine_rows,
            second_half * cosine_rows + first_half * sine_rows,
        ],
        axis=-1,
    )


def unrotate(grads, cosine, sine):
    half_dim = grads.shape[-1] // 2
    first_half = grads[..., :half_dim]
    second_half = grads[..., half_dim:]
    cosine_rows = cosine[:, None, :]
    sine_rows = sine[:, None, :]
    return jnp.concatenate(
        [
            first_half * cosine_rows + second_half * sine_rows,
            second_half * cosine_rows - first_half * sine_rows,
        ],
        axis=-1,
    )


def product(form, left, right):
    return jnp.einsum(form, left, right, preferred_element_type=jnp.float32)


def attend(queries, keys_in, values_in, upstream, segment_row, head_count, pair_count):
    length = queries.shape[0]
    group_size = head_count // pair_count
    cosine, sine, allowed = rope_tables(segment_row, DH)
    query_rot = (
        rotate(queries.reshape(length, head_count, DH), cosine, sine)
        .astype(jnp.bfloat16)
        .reshape(length, pair_count, group_size, DH)
    )
    key_rot = rotate(keys_in.reshape(length, pair_count, DH), cosine, sine).astype(jnp.bfloat16)
    value_heads = values_in.reshape(length, pair_count, DH).astype(jnp.bfloat16)
    factor = 1.0 / math.sqrt(DH)
    scores = product("tkgd,skd->kgts", query_rot, key_rot) * factor
    scores = jnp.where(allowed, scores, NEG_FILL)
    row_max = jnp.max(scores, axis=-1, keepdims=True)
    exponent = jnp.exp(scores - row_max)
    probs = exponent / jnp.sum(exponent, axis=-1, keepdims=True)
    probs_low = probs.astype(jnp.bfloat16)
    mixed = product("kgts,skd->tkgd", probs_low, value_heads).reshape(length, head_count * DH)
    cot_heads = upstream.reshape(length, pair_count, group_size, DH)
    prob_grad = product("tkgd,skd->kgts", cot_heads, value_heads)
    value_grad = product("kgts,tkgd->skd", probs_low, cot_heads)
    score_grad = probs * (prob_grad - jnp.sum(probs * prob_grad, axis=-1, keepdims=True))
    score_grad_low = score_grad.astype(jnp.bfloat16)
    query_grad = product("kgts,skd->tkgd", score_grad_low, key_rot) * factor
    key_grad = product("kgts,tkgd->skd", score_grad_low, query_rot) * factor
    query_grad = unrotate(query_grad.reshape(length, head_count, DH), cosine, sine).reshape(
        length, head_count * DH
    )
    key_grad = unrotate(key_grad, cosine, sine).reshape(length, pair_count * DH)
    return (
        mixed.astype(jnp.bfloat16),
        query_grad.astype(jnp.bfloat16),
        key_grad.astype(jnp.bfloat16),
        value_grad.reshape(length, pair_count * DH).astype(jnp.bfloat16),
    )


def row_total(values):
    return lax.psum(values, "tensor")


def token_sum(left, right):
    return lax.psum_scatter(
        lax.dot_general(
            left, right, (((0,), (0,)), ((), ())), preferred_element_type=jnp.float32
        ).astype(jnp.bfloat16),
        "fsdp",
        scatter_dimension=0,
        tiled=True,
    ).astype(jnp.float32)


def body(
    hidden,
    encoder_weight,
    decoder_weight,
    query_weight,
    key_weight,
    value_weight,
    segments,
    out_grad,
):
    residual = hidden[0]
    segment_row = segments[0, 0]
    upstream = out_grad[0]
    contract_last = (((1,), (1,)), ((), ()))
    encoder_rows, decoder_rows = (
        lax.all_gather(encoder_weight[0], "fsdp", axis=0, tiled=True),
        lax.all_gather(decoder_weight[0], "fsdp", axis=0, tiled=True),
    )
    code_partial = lax.dot_general(
        residual, encoder_rows, contract_last, preferred_element_type=jnp.float32
    )
    code_sent = lax.psum(code_partial, "tensor").astype(jnp.bfloat16)
    code_received = passed_along(code_sent, "section", 1)
    decoded = jnp.dot(code_received, decoder_rows, preferred_element_type=jnp.float32)
    norm_factor = lax.rsqrt(row_total(jnp.sum(decoded * decoded, axis=1)) / D + NORM_EPS)[:, None]
    normed = (decoded * norm_factor).astype(jnp.bfloat16)
    normed_full = lax.all_gather(normed, "tensor", axis=1, tiled=True)
    query_width = query_weight.shape[2]
    key_width = key_weight.shape[2]
    query_rows, key_rows, value_rows = (
        lax.all_gather(query_weight[0], "fsdp", axis=0, tiled=True),
        lax.all_gather(key_weight[0], "fsdp", axis=0, tiled=True),
        lax.all_gather(value_weight[0], "fsdp", axis=0, tiled=True),
    )
    queries = jnp.dot(normed_full, query_rows, preferred_element_type=jnp.float32)
    keys_all = jnp.dot(normed_full, key_rows, preferred_element_type=jnp.float32)
    values_all = jnp.dot(normed_full, value_rows, preferred_element_type=jnp.float32)
    mixed, query_grad, key_grad, value_grad = attend(
        queries, keys_all, values_all, upstream, segment_row, query_width // DH, key_width // DH
    )
    total = lax.dot_general(
        query_rows, query_grad, contract_last, preferred_element_type=jnp.float32
    )
    total = total + lax.dot_general(
        key_rows, key_grad, contract_last, preferred_element_type=jnp.float32
    )
    total = total + lax.dot_general(
        value_rows, value_grad, contract_last, preferred_element_type=jnp.float32
    )
    normed_grad = (
        lax.psum_scatter(total.astype(jnp.bfloat16), "tensor", scatter_dimension=0, tiled=True)
        .astype(jnp.float32)
        .T
    )
    inner_dot = row_total(jnp.sum(normed_grad * decoded, axis=1))[:, None]
    decoded_grad = (norm_factor * normed_grad - decoded * norm_factor**3 * inner_dot / D).astype(
        jnp.bfloat16
    )
    decoder_grad = token_sum(code_received, decoded_grad)
    code_grad_partial = lax.dot_general(
        decoded_grad, decoder_rows, contract_last, preferred_element_type=jnp.float32
    )
    code_grad_sent = lax.psum(code_grad_partial.astype(jnp.bfloat16), "tensor")
    code_grad = passed_along(code_grad_sent, "section", -1)
    encoder_grad = token_sum(code_grad, residual)
    hidden_grad = jnp.dot(code_grad, encoder_rows, preferred_element_type=jnp.float32).astype(
        jnp.bfloat16
    )
    return (mixed[None], hidden_grad[None], encoder_grad[None], decoder_grad[None])


def solution(mesh):
    placed = (
        P("section", "fsdp", "tensor"),
        P("section", "fsdp", "tensor"),
        P("section", "fsdp", "tensor"),
        P("section", "fsdp", "tensor"),
        P("section", "fsdp", "tensor"),
        P("section", "fsdp", "tensor"),
        P("section", "fsdp", None),
        P("section", "fsdp", "tensor"),
    )
    return jax.shard_map(
        body,
        mesh=mesh,
        in_specs=placed,
        out_specs=(
            P("section", "fsdp", "tensor"),
            P("section", "fsdp", "tensor"),
            P("section", "fsdp", "tensor"),
            P("section", "fsdp", "tensor"),
        ),
        check_vma=False,
    )
```

profile of v0, /device:TPU:1, one launch (start us, length us, event | category | flops | bytes accessed | tf_op | source)
XLA Modules:
  0.0 637.2 jit_solution(18349268483296418803)
XLA Ops:
  7.2 0.7 all-gather.14.cloned.1.call-update
  8.0 0.7 all-gather.16.cloned.1.call-update
  8.7 0.7 all-gather.20.cloned.1.call-update
  9.4 37.3 %all-gather.14.cloned.1.call-done = bf16[1,1024,1024]{2,1,0:T(8,128)(2,1)} async-done(((bf16[1,256,1024]{2,1,0:T(8,128)(2,1)}), bf16[1,1024,1024]{2,1,0:T(8,128)(2,1)}) %all-gather.14.cloned.1.call-update) | async-done | bytes 2097168 | tf_op jit(solution)/shard_map/all_gather | solution.py:138
  46.8 2.4 fusion.18
  49.2 38.5 %all-reduce.4 = bf16[128,1024]{1,0:T(8,128)(2,1)S(1)} all-reduce(f32[128,1024]{1,0:T(8,128)S(1)} %fusion.18), channel_id=1, replica_groups=mesh['section'=8,'fsdp'=4,'tensor'=8] {'tensor'}, use_global_device_ids=true, to_apply=%region_0.0 | all-reduce | flops 131072 | bytes 786432 | tf_op jit(solution)/shard_map/psum | solution.py:144
  87.7 8.9 %collective-permute-start = (bf16[128,1024]{1,0:T(8,128)(2,1)S(1)}, bf16[128,1024]{1,0:T(8,128)(2,1)S(1)}, u32[]{:S(2)}, u32[]{:S(2)}) collective-permute-start(bf16[128,1024]{1,0:T(8,128)(2,1)S(1)} %all-reduce.4), channel_id=1, source_target_pairs={{0,32},{32,64},{64,96},{96,128},{128,160},{160,192},{192,224},{224... | collective-permute-start | bytes 786440 | tf_op jit(solution)/shard_map/ppermute | solution.py:20
  96.6 4.6 collective-permute-done
  101.2 2.2 multiply_reduce_fusion.1
  103.5 15.4 %psum.29 = f32[128]{0:T(128)S(1)} all-reduce(f32[128]{0:T(128)S(1)} %get-tuple-element.26), channel_id=1, replica_groups=mesh['section'=8,'fsdp'=4,'tensor'=8] {'tensor'}, use_global_device_ids=true, to_apply=%region_2.0 | all-reduce | flops 128 | bytes 1024 | tf_op jit(solution)/shard_map/psum | solution.py:109
  118.9 0.5 multiply_multiply_fusion
  119.4 0.8 multiply_convert_fusion.1
  120.3 0.5 all-gather.18.cloned.1.call-update
  120.9 0.5 all-gather.22.cloned.1.call-update
  121.8 0.8 copy.47
  122.7 0.7 fusion.64
  123.4 0.3 multiply_cosine_fusion
  123.7 52.0 %all-gather.12.cloned.1.call-done = bf16[128,8192]{1,0:T(8,128)(2,1)} async-done(((bf16[128,1024]{1,0:T(8,128)(2,1)}), bf16[128,8192]{1,0:T(8,128)(2,1)}) %all-gather.12.cloned.1.call-update) | async-done | bytes 2097168 | tf_op jit(solution)/shard_map/all_gather | solution.py:149
  175.7 3.3 fusion.35
  179.0 0.8 fusion.84
  179.8 30.6 %all-gather.18.cloned.1.call-done = bf16[1,8192,128]{2,1,0:T(8,128)(2,1)} async-done(((bf16[1,2048,128]{2,1,0:T(8,128)(2,1)}), bf16[1,8192,128]{2,1,0:T(8,128)(2,1)}) %all-gather.18.cloned.1.call-update) | async-done | bytes 2097168 | tf_op jit(solution)/shard_map/all_gather | solution.py:155
  210.4 2.9 fusion.44
  213.3 155.4 %all-gather.22.cloned.1.call-done = bf16[1,8192,1024]{2,1,0:T(8,128)(2,1)} async-done(((bf16[1,2048,1024]{2,1,0:T(8,128)(2,1)}), bf16[1,8192,1024]{2,1,0:T(8,128)(2,1)}) %all-gather.22.cloned.1.call-update) | async-done | bytes 16777232 | tf_op jit(solution)/shard_map/all_gather | solution.py:153
  368.7 8.1 %fusion.22 = f32[16,8,8,128]{3,1,2,0:T(8,128)S(1)} fusion(bf16[128,8192]{1,0:T(8,128)(2,1)S(1)} %copy-done.1, bf16[1,8192,1024]{2,1,0:T(8,128)(2,1)} %all-gather.22.cloned.1.call-done), kind=kOutput, calls=%fused_computation.29 | convolution fusion | flops 2147483648 | bytes 19398656 | tf_op jit(solution)/shard_map/dot_general | solution.py:157
  377.7 0.3 fusion.95
  378.6 0.4 fusion.39
  379.0 0.3 fusion.20
  379.3 0.8 fusion.78
  380.5 0.9 copy.31
  381.4 13.7 %fusion = f32[128,8192]{1,0:T(8,128)} fusion(bf16[128,1024]{0,1:T(8,128)(2,1)} %bitcast.152, bf16[1,8192,1024]{2,1,0:T(8,128)(2,1)} %all-gather.22.cloned.1.call-done), kind=kOutput, calls=%fused_computation | convolution fusion | flops 2147483648 | bytes 21233664 | tf_op jit(solution)/shard_map/dot_general | solution.py:163
  395.1 4.9 convolution_add_fusion.1
  399.9 5.4 fusion.5
  405.4 56.1 %reduce-scatter.4.cloned.1.call-done = bf16[1024,128]{0,1:T(8,128)(2,1)} async-done(((bf16[8192,128]{0,1:T(8,128)(2,1)}), bf16[1024,128]{0,1:T(8,128)(2,1)}) %reduce-scatter.4.cloned.1.call-update) | async-done | bytes 262160 | tf_op jit(solution)/shard_map/reduce_scatter | solution.py:173
  461.5 1.1 fusion.49
  462.6 13.3 %psum.30 = f32[128]{0:T(128)S(1)} all-reduce(f32[128]{0:T(128)S(1)} %fusion.49), channel_id=1, replica_groups=mesh['section'=8,'fsdp'=4,'tensor'=8] {'tensor'}, use_global_device_ids=true, to_apply=%region_9.10 | all-reduce | flops 128 | bytes 1024 | tf_op jit(solution)/shard_map/psum | solution.py:109
  475.9 2.5 fusion.28
  478.5 3.2 convolution_convert_fusion
  481.8 73.3 %all-reduce.3.cloned.1.call-done = bf16[128,1024]{1,0:T(8,128)(2,1)} async-done(((bf16[128,1024]{1,0:T(8,128)(2,1)}), bf16[128,1024]{1,0:T(8,128)(2,1)}) %all-reduce.3.cloned.1.call-update) | async-done | bytes 262160 | tf_op jit(solution)/shard_map/psum | solution.py:185
  555.1 6.0 collective-permute-start.1
  561.1 7.7 %collective-permute-done.1 = bf16[128,1024]{1,0:T(8,128)(2,1)S(1)} collective-permute-done((bf16[128,1024]{1,0:T(8,128)(2,1)}, bf16[128,1024]{1,0:T(8,128)(2,1)S(1)}, u32[]{:S(2)}, u32[]{:S(2)}) %collective-permute-start.1) | collective-permute-done | bytes 262176 | tf_op jit(solution)/shard_map/ppermute | solution.py:20
  568.8 2.0 convolution_convert_fusion.1
  571.1 0.9 copy.34
  572.0 0.5 copy-done.3
  572.5 1.2 fusion.32
  573.7 20.1 %reduce-scatter.8.cloned.1.call-done = bf16[256,1024]{1,0:T(8,128)(2,1)} async-done(((bf16[1024,1024]{1,0:T(8,128)(2,1)}), bf16[256,1024]{1,0:T(8,128)(2,1)}) %reduce-scatter.8.cloned.1.call-update) | async-done | bytes 524304 | tf_op jit(solution)/shard_map/reduce_scatter | solution.py:113
  593.8 2.1 bitcast_convert_fusion
  596.0 32.3 %reduce-scatter.6.cloned.1.call-done = bf16[256,1024]{1,0:T(8,128)(2,1)} async-done(((bf16[1024,1024]{1,0:T(8,128)(2,1)}), bf16[256,1024]{1,0:T(8,128)(2,1)}) %reduce-scatter.6.cloned.1.call-update) | async-done | bytes 524304 | tf_op jit(solution)/shard_map/reduce_scatter | solution.py:113
  628.3 2.1 bitcast_convert_fusion.1
  (78 shorter events, 3.0 us)
Async XLA Ops:
  7.2 39.6 %copy-start = (bf16[1,128,1024]{2,1,0:T(8,128)(2,1)S(1)}, bf16[1,128,1024]{2,1,0:T(8,128)(2,1)}, u32[]{:S(2)}) copy-start(bf16[1,128,1024]{2,1,0:T(8,128)(2,1)} %param.8) | copy-start | bytes 786436
  7.2 39.6 %all-gather.14.cloned.1.call-start = ((), (), s32[]{:S(2)}) async-start(), calls=%async_computation.8 | async-start | bytes 2621440 | tf_op jit(solution)/shard_map/all_gather | solution.py:138
  7.9 88.7 %all-gather.16.cloned.1.call-start = ((), (), s32[]{:S(2)}) async-start(), calls=%async_computation.9 | async-start | bytes 2621440 | tf_op jit(solution)/shard_map/all_gather | solution.py:139
  8.7 115.0 %all-gather.20.cloned.1.call-start = ((), (), s32[]{:S(2)}) async-start(), calls=%async_computation.11 | async-start | bytes 2621440 | tf_op jit(solution)/shard_map/all_gather | solution.py:154
  9.4 166.3 %all-gather.12.cloned.1.call-start = ((), (), s32[]{:S(2)}) async-start(), calls=%async_computation.3 | async-start | bytes 2359296 | tf_op jit(solution)/shard_map/all_gather | solution.py:149
  87.7 13.6 %collective-permute-start = (bf16[128,1024]{1,0:T(8,128)(2,1)S(1)}, bf16[128,1024]{1,0:T(8,128)(2,1)S(1)}, u32[]{:S(2)}, u32[]{:S(2)}) collective-permute-start(bf16[128,1024]{1,0:T(8,128)(2,1)S(1)} %all-reduce.4), channel_id=1, source_target_pairs={{0,32},{32,64},{64,96},{96,128},{128,160},{160,192},{192,224},{224... | collective-permute-start | bytes 786440 | tf_op jit(solution)/shard_map/ppermute | solution.py:20
  101.2 19.6 %copy-start.5 = (bf16[128,1024]{1,0:T(8,128)(2,1)}, bf16[128,1024]{1,0:T(8,128)(2,1)S(1)}, u32[]{:S(2)}) copy-start(bf16[128,1024]{1,0:T(8,128)(2,1)S(1)} %collective-permute-done) | copy-start | bytes 786436
  119.4 0.9 copy-start.21
  120.2 90.2 %all-gather.18.cloned.1.call-start = ((), (), s32[]{:S(2)}) async-start(), calls=%async_computation.10 | async-start | bytes 2621440 | tf_op jit(solution)/shard_map/all_gather | solution.py:155
  120.8 1.0 copy-start.7
  120.8 1.7 copy-start.24
  120.9 247.9 %all-gather.22.cloned.1.call-start = ((), (), s32[]{:S(2)}) async-start(), calls=%async_computation.12 | async-start | bytes 20971520 | tf_op jit(solution)/shard_map/all_gather | solution.py:153
  121.4 340.1 %reduce-scatter.4.cloned.1.call-start = ((), (), s32[]{:S(2)}) async-start(), calls=%async_computation.4 | async-start | bytes 2359296 | tf_op jit(solution)/shard_map/reduce_scatter | solution.py:173
  122.5 56.5 %copy-start.17 = (f32[64]{0:T(128)}, f32[64]{0:T(128)S(1)}, u32[]{:S(2)}) copy-start(f32[64]{0:T(128)S(1)} %multiply_exponential_fusion) | copy-start | bytes 772
  122.7 56.4 %copy-start.19 = (f32[128]{0:T(128)}, f32[128]{0:T(128)S(1)}, u32[]{:S(2)}) copy-start(f32[128]{0:T(128)S(1)} %subtract_convert_fusion.2) | copy-start | bytes 1540
  175.7 34.7 %copy-start.1 = (bf16[128,8192]{1,0:T(8,128)(2,1)S(1)}, bf16[128,8192]{1,0:T(8,128)(2,1)}, u32[]{:S(2)}) copy-start(bf16[128,8192]{1,0:T(8,128)(2,1)} %all-gather.12.cloned.1.call-done) | copy-start | bytes 6291460
  376.9 0.7 copy-start.8
  376.9 0.7 copy-start.12
  377.2 1.0 copy-start.6
  377.2 1.0 copy-start.15
  378.0 0.6 copy-start.9
  378.1 0.9 copy-start.13
  378.4 0.9 copy-start.18
  378.4 0.9 copy-start.20
  381.4 13.7 %copy-start.2 = (bf16[1,8192,128]{2,1,0:T(8,128)(2,1)S(1)}, bf16[1,8192,128]{2,1,0:T(8,128)(2,1)}, u32[]{:S(2)}) copy-start(bf16[1,8192,128]{2,1,0:T(8,128)(2,1)} %all-gather.20.cloned.1.call-done) | copy-start | bytes 6291460
  381.4 13.7 %copy-start.11 = (bf16[128,1,64]{0,2,1:T(8,128)(2,1)S(1)}, bf16[128,1,64]{0,2,1:T(8,128)(2,1)}, u32[]{:S(2)}) copy-start(bf16[128,1,64]{0,2,1:T(8,128)(2,1)} %get-tuple-element.19) | copy-start | bytes 49156
  395.1 4.9 copy-start.10
  395.1 4.9 copy-start.14
  405.3 70.6 %copy-start.4 = (bf16[1,1024,1024]{2,1,0:T(8,128)(2,1)S(1)}, bf16[1,1024,1024]{2,1,0:T(8,128)(2,1)}, u32[]{:S(2)}) copy-start(bf16[1,1024,1024]{2,1,0:T(8,128)(2,1)} %all-gather.16.cloned.1.call-done) | copy-start | bytes 6291460
  405.3 70.6 %copy-start.22 = (f32[128]{0:T(128)S(1)}, f32[128]{0:T(128)}, u32[]{:S(2)}) copy-start(f32[128]{0:T(128)} %copy-done.21) | copy-start | bytes 1540
  405.3 70.6 %copy-start.23 = (f32[128]{0:T(128)S(1)}, f32[128]{0:T(128)}, u32[]{:S(2)}) copy-start(f32[128]{0:T(128)} %get-tuple-element.24) | copy-start | bytes 1540
  405.4 149.7 %all-reduce.3.cloned.1.call-start = ((), (), s32[]{:S(2)}) async-start(), calls=%async_computation.5 | async-start | bytes 524288 | tf_op jit(solution)/shard_map/psum | solution.py:185
  478.5 115.4 %reduce-scatter.8.cloned.1.call-start = ((), (), s32[]{:S(2)}) async-start(), calls=%async_computation.7 | async-start | bytes 2621440 | tf_op jit(solution)/shard_map/reduce_scatter | solution.py:113
  481.8 89.1 %copy-start.16 = (bf16[128,128,1]{1,0,2:T(8,128)(2,1)S(1)}, bf16[128,128,1]{1,0,2:T(8,128)(2,1)}, u32[]{:S(2)}) copy-start(bf16[128,128,1]{1,0,2:T(8,128)(2,1)} %fusion.44) | copy-start | bytes 98308
  481.8 146.5 %reduce-scatter.6.cloned.1.call-start = ((), (), s32[]{:S(2)}) async-start(), calls=%async_computation.6 | async-start | bytes 2621440 | tf_op jit(solution)/shard_map/reduce_scatter | solution.py:113
  555.1 13.7 %collective-permute-start.1 = (bf16[128,1024]{1,0:T(8,128)(2,1)}, bf16[128,1024]{1,0:T(8,128)(2,1)S(1)}, u32[]{:S(2)}, u32[]{:S(2)}) collective-permute-start(bf16[128,1024]{1,0:T(8,128)(2,1)} %all-reduce.3.cloned.1.call-done), channel_id=1, source_target_pairs={{0,224},{32,0},{64,32},{96,64},{128,96},{160,128},{192,160},{224,1... | collective-permute-start | bytes 786440 | tf_op jit(solution)/shard_map/ppermute | solution.py:20
  570.9 1.7 copy-start.3
Sparse Core Ops, SparseCore 0:
  9.8 36.9 all-gather.13
  48.6 33.3 all-gather.15
  83.8 33.3 all-gather.19
  120.4 55.3 all-gather.11
  177.4 32.9 all-gather.17
  212.1 156.6 all-gather.21
  405.5 55.9 reduce-scatter.3
  478.6 76.4 all-reduce.2
  557.7 36.1 reduce-scatter.7
  596.2 31.9 reduce-scatter.5
where the time goes:
time: 638 us; the launch traced here: 637 us
  waiting for transfers between devices  473 us (74%)
  blocking collectives  67.2 us (11%)
  matrix products  53.3 us (8%)
  starting transfers between devices  15.5 us (2%)
  between operations  14.5 us (2%)
  other arithmetic  10.2 us (2%)
    all_gather x1, waiting for transfers between devices, body(): lax.all_gather(query_weight[0], 'fsdp', axis=0, tiled=True)  155 us
    psum x1, waiting for transfers between devices, body(): code_grad_sent = lax.psum(code_grad_partial.astype(jnp.bfloat16), 'tensor')  73.3 us
    reduce_scatter x1, waiting for transfers between devices, body(): lax.psum_scatter(total.astype(jnp.bfloat16), 'tensor', scatter_dimension=...  56.1 us
    reduce_scatter x2, waiting for transfers between devices, token_sum(): lax.psum_scatter(lax.dot_general(left, right, (((0,), (0,)), ((), ())), p...  52.5 us
    all_gather x1, waiting for transfers between devices, body(): normed_full = lax.all_gather(normed, 'tensor', axis=1, tiled=True)  52 us
    psum x1, blocking collectives, body(): code_sent = lax.psum(code_partial, 'tensor').astype(jnp.bfloat16)  38.5 us
    all_gather x1, waiting for transfers between devices, body(): lax.all_gather(encoder_weight[0], 'fsdp', axis=0, tiled=True)  37.3 us
    all_gather x1, waiting for transfers between devices, body(): lax.all_gather(value_weight[0], 'fsdp', axis=0, tiled=True)  30.6 us
  transfers between devices with their start and end apart: 12, of which 10 were waited for; matrix products, arithmetic and copies ran while one was open for 4% of the time, Pallas kernels for 0%

commit v1 on v0

v1 whole, which is shorter than its diff:
```python
import math

import jax
import jax.numpy as jnp
from jax import lax
from jax.sharding import PartitionSpec as P


D = 8192
DH = 128
F = 4
T = 8
NORM_EPS = 1e-05
ROPE_BASE = 500000.0
NEG_FILL = -1e30
FT = ("fsdp", "tensor")
LOW = jnp.bfloat16
WIDE = jnp.float32


def exchange(blocks, axis):
    return lax.all_to_all(blocks, axis, 0, 0)


def spread(value, axis, count):
    return exchange(jnp.broadcast_to(value[None], (count,) + value.shape), axis)


def to_section(value, steps):
    return lax.ppermute(value, "section", [(i, (i + steps) % 8) for i in range(8)])


def column_route(turn):
    pairs = []
    for f in range(F):
        for t in range(T):
            target = (t // 2) * T + 4 * (t % 2) + (f + turn) % 4
            pairs.append((f * T + t, target))
    return pairs


def dot(left, right, left_dim, right_dim):
    return lax.dot_general(
        left, right, (((left_dim,), (right_dim,)), ((), ())), preferred_element_type=WIDE
    )


def split(values):
    high = values.astype(LOW)
    low = (values - high.astype(WIDE)).astype(LOW)
    return high, low


def rope_tables(segment_row, dim):
    length = segment_row.shape[0]
    positions = jnp.arange(length, dtype=jnp.int32)
    earlier = jnp.sum((segment_row[None, :] < segment_row[:, None]).astype(jnp.int32), axis=1)
    places = (positions - earlier).astype(WIDE)
    frequency = jnp.exp(jnp.arange(0, dim, 2).astype(WIDE) * (-math.log(ROPE_BASE) / dim))
    angles = places[:, None] * frequency[None, :]
    allowed = (segment_row[None, :] == segment_row[:, None]) & (
        positions[None, :] <= positions[:, None]
    )
    return jnp.cos(angles), jnp.sin(angles), allowed


def rotate(values, cosine, sine):
    half = DH // 2
    first, second = values[..., :half], values[..., half:]
    cos_rows, sin_rows = cosine[:, None, :], sine[:, None, :]
    return jnp.concatenate(
        [first * cos_rows - second * sin_rows, second * cos_rows + first * sin_rows], axis=-1
    )


def product(form, left, right):
    return jnp.einsum(form, left, right, preferred_element_type=WIDE)


def attend(queries, keys, values, upstream, tables):
    length, width = queries.shape
    heads = width // DH
    cosine, sine, allowed = tables
    factor = 1.0 / math.sqrt(DH)
    query_rot = rotate(queries.reshape(length, heads, DH), cosine, sine).astype(LOW)
    key_rot = rotate(keys[:, None], cosine, sine)[:, 0].astype(LOW)
    value_low = values.astype(LOW)
    upstream = upstream.reshape(length, heads, DH)
    scores = product("tgd,sd->gts", query_rot, key_rot) * factor
    scores = jnp.where(allowed, scores, NEG_FILL)
    exponent = jnp.exp(scores - jnp.max(scores, axis=-1, keepdims=True))
    probs = exponent / jnp.sum(exponent, axis=-1, keepdims=True)
    probs_low = probs.astype(LOW)
    mixed = product("gts,sd->tgd", probs_low, value_low).reshape(length, width)
    prob_grad = product("tgd,sd->gts", upstream, value_low)
    value_grad = product("gts,tgd->sd", probs_low, upstream)
    score_grad = probs * (prob_grad - jnp.sum(probs * prob_grad, axis=-1, keepdims=True))
    score_grad = score_grad.astype(LOW)
    query_grad = product("gts,sd->tgd", score_grad, key_rot) * factor
    key_grad = product("gts,tgd->sd", score_grad, query_rot) * factor
    query_grad = rotate(query_grad, cosine, -sine).reshape(length, width)
    key_grad = rotate(key_grad[:, None], cosine, -sine)[:, 0]
    return mixed.astype(LOW), query_grad, key_grad, value_grad


def section_step(
    hidden,
    encoder_weight,
    decoder_weight,
    query_weight,
    key_weight,
    value_weight,
    segments,
    out_grad,
):
    f = lax.axis_index("fsdp")
    t = lax.axis_index("tensor")
    encoder = encoder_weight[0]
    decoder = decoder_weight[0]

    columns = decoder.reshape(256, 4, 256)
    decoder_cols = jnp.zeros((F, 256, 256), LOW)
    for turn in range(F):
        block = lax.dynamic_index_in_dim(columns, (f + turn) % 4, 1, keepdims=False)
        came = lax.ppermute(block, FT, column_route(turn))
        decoder_cols = lax.dynamic_update_index_in_dim(
            decoder_cols, came, (t + 4 - turn) % 4, 0
        )
    decoder_cols = decoder_cols.reshape(1024, 256)

    hidden_all = spread(hidden[0], "fsdp", F).reshape(512, 1024)
    encoder, hidden_all = lax.optimization_barrier((encoder, hidden_all))

    encoder_parts = [encoder]
    for turn in range(1, F):
        pairs = [(i, (i + turn) % F) for i in range(F)]
        encoder_parts.append(lax.ppermute(encoder, "fsdp", pairs))

    code_part = dot(hidden_all, encoder, 1, 1).astype(LOW).reshape(T, 64, 256)
    code_piece = jnp.sum(exchange(code_part, "tensor").astype(WIDE), axis=0).astype(LOW)
    code_moved = to_section(code_piece, 1)
    pieces = spread(code_moved, FT, F * T).reshape(F, 512, 256)
    code_in = jnp.concatenate([pieces[i] for i in range(F)], axis=1)

    decoded = dot(code_in, decoder_cols, 1, 0)
    gathered = spread(decoded.astype(LOW), "tensor", T)

    weights = jnp.concatenate([query_weight[0], key_weight[0], value_weight[0]], axis=1)
    tables = rope_tables(segments[0, 0], DH)
    decoded_low = jnp.concatenate([gathered[i] for i in range(T)], axis=1)
    squares = jnp.sum(jnp.square(decoded_low.astype(WIDE)), axis=1)[:, None]
    square_high, square_low = split(squares)
    part = dot(decoded_low, weights, 1, 0).astype(LOW)
    lane = lax.broadcasted_iota(jnp.int32, (512, 128), 1)
    extra = jnp.where(lane == 0, square_high, jnp.where(lane == 1, square_low, 0))
    sent = jnp.concatenate([part, extra], axis=1).reshape(F, 128, 1408)
    total = jnp.sum(exchange(sent, "fsdp").astype(WIDE), axis=0)
    norm_factor = lax.rsqrt((total[:, 1280:1281] + total[:, 1281:1282]) / D + NORM_EPS)
    queries = total[:, :1024] * norm_factor
    keys = total[:, 1024:1152] * norm_factor
    values = total[:, 1152:1280] * norm_factor

    mixed, query_grad, key_grad, value_grad = attend(
        queries, keys, values, out_grad[0], tables
    )
    weight = (
        jnp.sum(queries * query_grad, axis=1)
        + jnp.sum(keys * key_grad, axis=1)
        + jnp.sum(values * value_grad, axis=1)
    )[:, None]
    weight_high, weight_low = split(weight * jnp.square(norm_factor) / D)
    lane = lane[:128]
    extra = jnp.where(lane == 0, weight_high, jnp.where(lane == 1, weight_low, 0))
    sent = jnp.concatenate(
        [
            (query_grad * norm_factor).astype(LOW),
            (key_grad * norm_factor).astype(LOW),
            (value_grad * norm_factor).astype(LOW),
            extra,
        ],
        axis=1,
    )
    grads = spread(sent, "fsdp", F).reshape(512, 1408)
    radial = grads[:, 1280:1281].astype(WIDE) + grads[:, 1281:1282].astype(WIDE)

    share = dot(grads[:, :1280], weights, 1, 1) - decoded_low.astype(WIDE) * radial
    share = share.astype(LOW)

    share = share.reshape(512, T, 256).transpose(1, 0, 2)
    decoded_grad = jnp.sum(exchange(share, "tensor").astype(WIDE), axis=0).astype(LOW)

    code_share = dot(decoded_grad, decoder_cols, 1, 1).astype(LOW)
    code_share = code_share.reshape(T, 64, F, 256).transpose(2, 0, 1, 3).reshape(F * T, 64, 256)
    grad_piece = jnp.sum(exchange(code_share, FT).astype(WIDE), axis=0).astype(LOW)
    grad_moved = to_section(grad_piece, -1)

    decoder_part = dot(code_in, decoded_grad, 0, 0).astype(LOW).reshape(F, 256, 256)
    came = []
    for turn in range(F):
        block = lax.dynamic_index_in_dim(decoder_part, (t + 4 - turn) % 4, 0, keepdims=False)
        back = [(target, source) for source, target in column_route(turn)]
        came.append(lax.ppermute(block, FT, back))

    grad_pieces = spread(grad_moved, FT, F * T).reshape(F, 512, 256)
    code_grad_cols = lax.dynamic_index_in_dim(grad_pieces, f, 0, keepdims=False)
    code_grad_rows = lax.dynamic_slice_in_dim(grad_pieces, f * 128, 128, 1)
    encoder_grad = dot(code_grad_cols, hidden_all, 0, 0)
    hidden_grad = jnp.zeros((128, 1024), WIDE)
    for turn in range(F):
        part = lax.dynamic_index_in_dim(code_grad_rows, (f + 4 - turn) % 4, 0, keepdims=False)
        hidden_grad = hidden_grad + dot(part, encoder_parts[turn], 1, 0)

    came = jnp.stack(came)
    decoder_grad = jnp.concatenate(
        [
            lax.dynamic_index_in_dim(came, (c + 4 - f) % 4, 0, keepdims=False)
            for c in range(4)
        ],
        axis=1,
    ).astype(WIDE)
    return (
        mixed[None],
        hidden_grad.astype(LOW)[None],
        encoder_grad[None],
        decoder_grad[None],
    )


def solution(mesh):
    placed = P("section", "fsdp", "tensor")
    return jax.shard_map(
        section_step,
        mesh=mesh,
        in_specs=(placed,) * 6 + (P("section", "fsdp", None), placed),
        out_specs=(placed,) * 4,
        check_vma=False,
    )
```

time: 638 us -> 311 us (0.49)
  waiting for transfers between devices: 473 us -> 82.1 us
  starting transfers between devices: 15.5 us -> 75.4 us
  blocking collectives: 67.2 us -> 100 us
  matrix products: 53.3 us -> 21.7 us
  between operations: 14.5 us -> 1.71 us
  local copies, waits for them, and re-layouts: 3.85 us -> 16.2 us
    all_gather x6 -> x0, waiting for transfers between devices: 275 us -> none  [the longest x1 155 us: body(): lax.all_gather(query_weight[0], 'fsdp', axis=0, tiled=True)]
    reduce_scatter x3 -> x0, waiting for transfers between devices: 109 us -> none  [the longest x1 56.1 us: body(): lax.psum_scatter(total.astype(jnp.bfloat16), 'tensor', scatter_dimension=...]
    all_to_all x0 -> x5, blocking collectives: none -> 100 us  [exchange(): return lax.all_to_all(blocks, axis, 0, 0)]
    psum x1 -> x0, waiting for transfers between devices: 73.3 us -> none  [body(): code_grad_sent = lax.psum(code_grad_partial.astype(jnp.bfloat16), 'tensor')]
    psum x3 -> x0, blocking collectives: 67.2 us -> none  [the longest x1 38.5 us: body(): code_sent = lax.psum(code_partial, 'tensor').astype(jnp.bfloat16)]
    all_to_all x0 -> x4, waiting for transfers between devices: none -> 42.2 us  [exchange(): return lax.all_to_all(blocks, axis, 0, 0)]
    ppermute x2 -> x13, starting transfers between devices: 14.9 us -> 55.6 us  [the longest x3 20.7 us: section_step(): encoder_parts.append(lax.ppermute(encoder, 'fsdp', pairs))]
    dot_general x17 -> x16, matrix products: 53.3 us -> 21.3 us  [the longest x11 18.5 us: dot(): lax.dot_general(left, right, (((left_dim,), (right_dim,)), ((), ())), pre...]
  transfers between devices with their start and end apart: 12 -> 17, of which waited for: 10 -> 8; matrix products, arithmetic and copies ran while one was open for 4% -> 4% of each run, Pallas kernels for 0% -> 0%
where the time goes in v1:
time: 311 us; the launch traced here: 306 us
  blocking collectives  100 us (32%)
  waiting for transfers between devices  82.1 us (26%)
  starting transfers between devices  75.4 us (24%)
  matrix products  21.7 us (7%)
  local copies, waits for them, and re-layouts  16.2 us (5%)
  other arithmetic  9.19 us (3%)
    all_to_all x5, blocking collectives, exchange(): return lax.all_to_all(blocks, axis, 0, 0)  100 us
    all_to_all x4, waiting for transfers between devices, exchange(): return lax.all_to_all(blocks, axis, 0, 0)  42.2 us
    ppermute x3, starting transfers between devices, section_step(): encoder_parts.append(lax.ppermute(encoder, 'fsdp', pairs))  20.7 us
    all_to_all x4, starting transfers between devices, exchange(): return lax.all_to_all(blocks, axis, 0, 0)  19.9 us
    dot_general x11, matrix products, dot(): lax.dot_general(left, right, (((left_dim,), (right_dim,)), ((), ())), pre...  18.5 us
    ppermute x4, waiting for transfers between devices, section_step(): came = lax.ppermute(block, FT, column_route(turn))  17.7 us
    ppermute x4, starting transfers between devices, section_step(): came = lax.ppermute(block, FT, column_route(turn))  15.3 us
    ppermute x3, waiting for transfers between devices, section_step(): encoder_parts.append(lax.ppermute(encoder, 'fsdp', pairs))  15.1 us
  transfers between devices with their start and end apart: 17, of which 8 were waited for; matrix products, arithmetic and copies ran while one was open for 4% of the time, Pallas kernels for 0%

profile of v1, /device:TPU:1, one launch (start us, length us, event | category | flops | bytes accessed | tf_op | source)
XLA Modules:
  0.0 306.4 jit_solution(16741080794745297538)
XLA Ops:
  0.6 1.1 broadcast_in_dim.131
  1.8 18.8 %all_to_all.45 = bf16[4,128,1024]{2,1,0:T(8,128)(2,1)S(1)} all-to-all(bf16[4,128,1024]{2,1,0:T(8,128)(2,1)S(1)} %broadcast_in_dim.131), channel_id=1, replica_groups=mesh['section'=8,'fsdp'=4,'tensor'=8] {'fsdp'}, dimensions={0} | all-to-all | bytes 2097152 | tf_op jit(solution)/shard_map/all_to_all | solution.py:22
  20.6 1.0 copy-done
  22.1 11.6 %all_to_all.46 = bf16[8,64,256]{2,1,0:T(8,128)(2,1)S(1)} all-to-all(bf16[8,64,256]{2,1,0:T(8,128)(2,1)S(1)} %bitcast.235), channel_id=1, replica_groups=mesh['section'=8,'fsdp'=4,'tensor'=8] {'tensor'}, dimensions={0} | all-to-all | bytes 524288 | tf_op jit(solution)/shard_map/all_to_all | solution.py:22
  33.8 6.2 %collective-permute-start = (bf16[64,256]{1,0:T(8,128)(2,1)S(1)}, bf16[64,256]{1,0:T(8,128)(2,1)S(1)}, u32[]{:S(2)}, u32[]{:S(2)}) collective-permute-start(bf16[64,256]{1,0:T(8,128)(2,1)S(1)} %reduce_sum.108), channel_id=1, source_target_pairs={{0,32},{32,64},{64,96},{96,128},{128,160},{160,192},{192,224},{224... | collective-permute-start | bytes 98312 | tf_op jit(solution)/shard_map/ppermute | solution.py:30
  40.0 1.0 collective-permute-done
  41.0 1.1 broadcast_in_dim.132
  42.1 3.9 %all-to-all-start.2 = ((bf16[32,64,256]{2,1,0:T(8,128)(2,1)}), bf16[32,64,256]{2,1,0:T(8,128)(2,1)S(1)}, u32[]{:S(2)}, u32[]{:S(2)}) async-start(bf16[32,64,256]{2,1,0:T(8,128)(2,1)} %broadcast_in_dim.132), calls=%async_computation.2 | async-start | bytes 2097152 | tf_op jit(solution)/shard_map/all_to_all | solution.py:22
  47.2 7.0 %collective-permute-start.2 = (bf16[256,256]{1,0:T(8,128)(2,1)S(1)}, bf16[256,256]{1,0:T(8,128)(2,1)S(1)}, u32[]{:S(2)}, u32[]{:S(2)}) collective-permute-start(bf16[256,256]{1,0:T(8,128)(2,1)S(1)} %bitcast.246), channel_id=1, source_target_pairs={{0,1},{1,5},{2,9},{3,13},{4,17},{5,21},{6,25},{7,29},{8,2},{9,6},{... | collective-permute-start | bytes 393224 | tf_op jit(solution)/shard_map/ppermute | solution.py:125
  54.3 2.2 collective-permute-start.3
  56.6 5.5 %collective-permute-start.4 = (bf16[256,256]{1,0:T(8,128)(2,1)S(1)}, bf16[256,256]{1,0:T(8,128)(2,1)S(1)}, u32[]{:S(2)}, u32[]{:S(2)}) collective-permute-start(bf16[256,256]{1,0:T(8,128)(2,1)S(1)} %bitcast.245), channel_id=1, source_target_pairs={{0,3},{1,7},{2,11},{3,15},{4,19},{5,23},{6,27},{7,31},{8,0},{9,4},... | collective-permute-start | bytes 393224 | tf_op jit(solution)/shard_map/ppermute | solution.py:125
  62.3 17.6 %collective-permute-done.2 = bf16[256,256]{1,0:T(8,128)(2,1)S(1)} collective-permute-done((bf16[256,256]{1,0:T(8,128)(2,1)S(1)}, bf16[256,256]{1,0:T(8,128)(2,1)S(1)}, u32[]{:S(2)}, u32[]{:S(2)}) %collective-permute-start.2) | collective-permute-done | bytes 131104 | tf_op jit(solution)/shard_map/ppermute | solution.py:125
  81.1 1.5 broadcast_in_dim.138
  82.6 8.1 %all-to-all-start.3 = ((bf16[8,512,256]{2,1,0:T(8,128)(2,1)}), bf16[8,512,256]{2,1,0:T(8,128)(2,1)S(1)}, u32[]{:S(2)}, u32[]{:S(2)}) async-start(bf16[8,512,256]{2,1,0:T(8,128)(2,1)} %broadcast_in_dim.138), calls=%async_computation.3 | async-start | bytes 4194304 | tf_op jit(solution)/shard_map/all_to_all | solution.py:22
  90.7 25.7 %all-to-all-done.3 = bf16[8,512,256]{2,1,0:T(8,128)(2,1)S(1)} async-done(((bf16[8,512,256]{2,1,0:T(8,128)(2,1)}), bf16[8,512,256]{2,1,0:T(8,128)(2,1)S(1)}, u32[]{:S(2)}, u32[]{:S(2)}) %all-to-all-start.3) | async-done | bytes 2097184 | tf_op jit(solution)/shard_map/all_to_all | solution.py:22
  117.9 1.9 copy-done.24
  119.8 2.9 convolution_convert_fusion
  123.0 1.2 pad_maximum_fusion.3
  124.2 3.9 %all-to-all-start.4 = ((bf16[4,128,1408]{2,1,0:T(8,128)(2,1)}), bf16[4,128,1408]{2,1,0:T(8,128)(2,1)S(1)}, u32[]{:S(2)}, u32[]{:S(2)}) async-start(bf16[4,128,1408]{2,1,0:T(8,128)(2,1)} %bitcast.29), calls=%async_computation.4 | async-start | bytes 2883584 | tf_op jit(solution)/shard_map/all_to_all | solution.py:22
  128.8 16.5 %all-to-all-done.4 = bf16[4,128,1408]{2,1,0:T(8,128)(2,1)S(1)} async-done(((bf16[4,128,1408]{2,1,0:T(8,128)(2,1)}), bf16[4,128,1408]{2,1,0:T(8,128)(2,1)S(1)}, u32[]{:S(2)}, u32[]{:S(2)}) %all-to-all-start.4) | async-done | bytes 1441824 | tf_op jit(solution)/shard_map/all_to_all | solution.py:22
  151.3 18.7 %all_to_all.47 = bf16[4,128,1408]{1,2,0:T(8,128)(2,1)S(1)} all-to-all(bf16[4,128,1408]{1,2,0:T(8,128)(2,1)S(1)} %broadcast_in_dim.151), channel_id=1, replica_groups=mesh['section'=8,'fsdp'=4,'tensor'=8] {'fsdp'}, dimensions={0} | all-to-all | bytes 2883584 | tf_op jit(solution)/shard_map/all_to_all | solution.py:22
  170.1 1.5 copy.186
  171.6 1.2 add_reduce_fusion
  172.8 6.5 %fusion.3 = bf16[512,2048]{1,0:T(8,128)(2,1)S(1)} fusion(bf16[512,2048]{1,0:T(8,128)(2,1)} %copy-done.2, bf16[2048,128]{1,0:T(8,128)(2,1)} %bitcast.253, bf16[2048,128]{1,0:T(8,128)(2,1)} %bitcast.255, bf16[2048,1024]{1,0:T(8,128)(2,1)} %bitcast.251, f32[512]{0:T(512)S(1)} %add_reduce_fusion, bf16[512,1408]{1,0:T(8,128)(2,1)} %bitcast.224), kind=kOutput, calls=%fused_computation.6 | convolution fusion | flops 2704277504 | bytes 10749952 | tf_op jit(solution)/shard_map/dot_general | solution.py:43
  179.4 31.1 %all_to_all.48 = bf16[8,512,256]{2,1,0:T(8,128)(2,1)S(1)} all-to-all(bf16[8,512,256]{2,1,0:T(8,128)(2,1)S(1)} %bitcast.208), channel_id=1, replica_groups=mesh['section'=8,'fsdp'=4,'tensor'=8] {'tensor'}, dimensions={0} | all-to-all | bytes 4194304 | tf_op jit(solution)/shard_map/all_to_all | solution.py:22
  210.6 1.0 reduce_sum.117
  211.6 1.4 convolution_convert_fusion.1
  214.0 19.7 %all_to_all.49 = bf16[32,64,256]{2,1,0:T(8,128)(2,1)S(1)} all-to-all(bf16[32,64,256]{2,1,0:T(8,128)(2,1)S(1)} %bitcast.211), channel_id=1, replica_groups=mesh['section'=8,'fsdp'=4,'tensor'=8] {'fsdp','tensor'}, dimensions={0} | all-to-all | bytes 2097152 | tf_op jit(solution)/shard_map/all_to_all | solution.py:22
  233.9 2.8 collective-permute-start.5
  236.7 5.4 %collective-permute-done.5 = bf16[64,256]{1,0:T(8,128)(2,1)S(1)} collective-permute-done((bf16[64,256]{1,0:T(8,128)(2,1)S(1)}, bf16[64,256]{1,0:T(8,128)(2,1)S(1)}, u32[]{:S(2)}, u32[]{:S(2)}) %collective-permute-start.5) | collective-permute-done | bytes 32800 | tf_op jit(solution)/shard_map/ppermute | solution.py:30
  242.2 1.1 broadcast_in_dim.152
  243.3 3.9 %all-to-all-start.8 = ((bf16[32,64,256]{2,1,0:T(8,128)(2,1)}), bf16[32,64,256]{2,1,0:T(8,128)(2,1)S(1)}, u32[]{:S(2)}, u32[]{:S(2)}) async-start(bf16[32,64,256]{2,1,0:T(8,128)(2,1)} %broadcast_in_dim.152), calls=%async_computation.8 | async-start | bytes 2097152 | tf_op jit(solution)/shard_map/all_to_all | solution.py:22
  247.3 2.8 collective-permute-start.8
  250.1 1.6 convolution_convert_fusion.2
  252.5 1.9 collective-permute-start.12
  254.4 3.2 %collective-permute-start.11 = (bf16[256,256]{1,0:T(8,128)(2,1)}, bf16[256,256]{1,0:T(8,128)(2,1)}, u32[]{:S(2)}, u32[]{:S(2)}) collective-permute-start(bf16[256,256]{1,0:T(8,128)(2,1)} %get-tuple-element.58), channel_id=1, source_target_pairs={{2,0},{6,1},{10,2},{14,3},{18,4},{22,5},{26,6},{30,7},{3,8},{7,9},... | collective-permute-start | bytes 393224 | tf_op jit(solution)/shard_map/ppermute | solution.py:202
  257.6 4.1 %collective-permute-start.10 = (bf16[256,256]{1,0:T(8,128)(2,1)S(1)}, bf16[256,256]{1,0:T(8,128)(2,1)}, u32[]{:S(2)}, u32[]{:S(2)}) collective-permute-start(bf16[256,256]{1,0:T(8,128)(2,1)S(1)} %get-tuple-element.59), channel_id=1, source_target_pairs={{1,0},{5,1},{9,2},{13,3},{17,4},{21,5},{25,6},{29,7},{2,8},{6,9},{... | collective-permute-start | bytes 393224 | tf_op jit(solution)/shard_map/ppermute | solution.py:202
  261.7 1.3 collective-permute-start.9
  263.0 1.3 convolution_convert_fusion.3
  265.1 2.4 collective-permute-start.6
  268.2 15.5 %collective-permute-start.7 = (bf16[256,1024]{1,0:T(8,128)(2,1)S(1)}, bf16[256,1024]{1,0:T(8,128)(2,1)S(1)}, u32[]{:S(2)}, u32[]{:S(2)}) collective-permute-start(bf16[256,1024]{1,0:T(8,128)(2,1)S(1)} %bitcast.228), channel_id=1, source_target_pairs={{0,16},{8,24},{16,0},{24,8},{1,17},{9,25},{17,1},{25,9},{2,18},{10... | collective-permute-start | bytes 1572872 | tf_op jit(solution)/shard_map/ppermute | solution.py:137
  283.7 1.1 pad_maximum_fusion.6
  284.9 1.1 maximum_convert_fusion
  286.4 1.4 convolution_bitcast_fusion
  287.8 1.3 fusion.42
  289.1 4.2 %collective-permute-done.6 = bf16[256,1024]{1,0:T(8,128)(2,1)} collective-permute-done((bf16[256,1024]{1,0:T(8,128)(2,1)S(1)}, bf16[256,1024]{1,0:T(8,128)(2,1)}, u32[]{:S(2)}, u32[]{:S(2)}) %collective-permute-start.6) | collective-permute-done | bytes 524320 | tf_op jit(solution)/shard_map/ppermute | solution.py:137
  293.3 1.3 convolution_add_fusion.1
  294.6 10.9 %collective-permute-done.7 = bf16[256,1024]{1,0:T(8,128)(2,1)S(1)} collective-permute-done((bf16[256,1024]{1,0:T(8,128)(2,1)S(1)}, bf16[256,1024]{1,0:T(8,128)(2,1)S(1)}, u32[]{:S(2)}, u32[]{:S(2)}) %collective-permute-start.7) | collective-permute-done | bytes 524320 | tf_op jit(solution)/shard_map/ppermute | solution.py:137
  (136 shorter events, 15.9 us)
Async XLA Ops:
  0.6 21.0 %copy-start.8 = (bf16[1,256,1024]{2,1,0:T(8,128)(2,1)S(1)}, bf16[1,256,1024]{2,1,0:T(8,128)(2,1)}, u32[]{:S(2)}) copy-start(bf16[1,256,1024]{2,1,0:T(8,128)(2,1)} %param.9) | copy-start | bytes 1572868
  20.6 1.0 copy-start
  22.1 24.0 %copy-start.10 = (bf16[1,256,1024]{2,1,0:T(8,128)(2,1)S(1)}, bf16[1,256,1024]{2,1,0:T(8,128)(2,1)}, u32[]{:S(2)}) copy-start(bf16[1,256,1024]{2,1,0:T(8,128)(2,1)} %param.10) | copy-start | bytes 1572868
  33.8 7.2 %collective-permute-start = (bf16[64,256]{1,0:T(8,128)(2,1)S(1)}, bf16[64,256]{1,0:T(8,128)(2,1)S(1)}, u32[]{:S(2)}, u32[]{:S(2)}) collective-permute-start(bf16[64,256]{1,0:T(8,128)(2,1)S(1)} %reduce_sum.108), channel_id=1, source_target_pairs={{0,32},{32,64},{64,96},{96,128},{128,160},{160,192},{192,224},{224... | collective-permute-start | bytes 98312 | tf_op jit(solution)/shard_map/ppermute | solution.py:30
  42.1 37.9 %all-to-all-start.2 = ((bf16[32,64,256]{2,1,0:T(8,128)(2,1)}), bf16[32,64,256]{2,1,0:T(8,128)(2,1)S(1)}, u32[]{:S(2)}, u32[]{:S(2)}) async-start(bf16[32,64,256]{2,1,0:T(8,128)(2,1)} %broadcast_in_dim.132), calls=%async_computation.2 | async-start | bytes 2097152 | tf_op jit(solution)/shard_map/all_to_all | solution.py:22
  46.5 15.7 %collective-permute-start.1 = (bf16[256,256]{1,0:T(8,128)(2,1)S(1)}, bf16[256,256]{1,0:T(8,128)(2,1)S(1)}, u32[]{:S(2)}, u32[]{:S(2)}) collective-permute-start(bf16[256,256]{1,0:T(8,128)(2,1)S(1)} %bitcast.247), channel_id=1, source_target_pairs={{0,0},{1,4},{2,8},{3,12},{4,16},{5,20},{6,24},{7,28},{8,1},{9,5},{... | collective-permute-start | bytes 393224 | tf_op jit(solution)/shard_map/ppermute | solution.py:125
  47.2 32.7 %collective-permute-start.2 = (bf16[256,256]{1,0:T(8,128)(2,1)S(1)}, bf16[256,256]{1,0:T(8,128)(2,1)S(1)}, u32[]{:S(2)}, u32[]{:S(2)}) collective-permute-start(bf16[256,256]{1,0:T(8,128)(2,1)S(1)} %bitcast.246), channel_id=1, source_target_pairs={{0,1},{1,5},{2,9},{3,13},{4,17},{5,21},{6,25},{7,29},{8,2},{9,6},{... | collective-permute-start | bytes 393224 | tf_op jit(solution)/shard_map/ppermute | solution.py:125
  54.3 25.6 %collective-permute-start.3 = (bf16[256,256]{1,0:T(8,128)(2,1)S(1)}, bf16[256,256]{1,0:T(8,128)(2,1)S(1)}, u32[]{:S(2)}, u32[]{:S(2)}) collective-permute-start(bf16[256,256]{1,0:T(8,128)(2,1)S(1)} %bitcast.244), channel_id=1, source_target_pairs={{0,2},{1,6},{2,10},{3,14},{4,18},{5,22},{6,26},{7,30},{8,3},{9,7},... | collective-permute-start | bytes 393224 | tf_op jit(solution)/shard_map/ppermute | solution.py:125
  56.6 23.4 %collective-permute-start.4 = (bf16[256,256]{1,0:T(8,128)(2,1)S(1)}, bf16[256,256]{1,0:T(8,128)(2,1)S(1)}, u32[]{:S(2)}, u32[]{:S(2)}) collective-permute-start(bf16[256,256]{1,0:T(8,128)(2,1)S(1)} %bitcast.245), channel_id=1, source_target_pairs={{0,3},{1,7},{2,11},{3,15},{4,19},{5,23},{6,27},{7,31},{8,0},{9,4},... | collective-permute-start | bytes 393224 | tf_op jit(solution)/shard_map/ppermute | solution.py:125
  80.1 0.7 copy-start.12
  80.1 0.8 copy-start.14
  80.2 0.9 copy-start.15
  80.2 1.0 copy-start.16
  82.6 33.8 %all-to-all-start.3 = ((bf16[8,512,256]{2,1,0:T(8,128)(2,1)}), bf16[8,512,256]{2,1,0:T(8,128)(2,1)S(1)}, u32[]{:S(2)}, u32[]{:S(2)}) async-start(bf16[8,512,256]{2,1,0:T(8,128)(2,1)} %broadcast_in_dim.138), calls=%async_computation.3 | async-start | bytes 4194304 | tf_op jit(solution)/shard_map/all_to_all | solution.py:22
  116.5 1.1 copy-start.26
  116.6 1.3 copy-start.25
  116.6 3.2 %copy-start.24 = (bf16[1,2048,1024]{2,1,0:T(8,128)(2,1)S(1)}, bf16[1,2048,1024]{2,1,0:T(8,128)(2,1)}, u32[]{:S(2)}) copy-start(bf16[1,2048,1024]{2,1,0:T(8,128)(2,1)} %param.11) | copy-start | bytes 12582916
  116.7 6.0 %copy-start.2 = (bf16[512,2048]{1,0:T(8,128)(2,1)}, bf16[512,2048]{1,0:T(8,128)(2,1)S(1)}, u32[]{:S(2)}) copy-start(bf16[512,2048]{1,0:T(8,128)(2,1)S(1)} %fusion.15) | copy-start | bytes 6291460
  124.2 3.9 %copy-start.11 = (bf16[1,128,1024]{2,1,0:T(8,128)(2,1)S(1)}, bf16[1,128,1024]{2,1,0:T(8,128)(2,1)}, u32[]{:S(2)}) copy-start(bf16[1,128,1024]{2,1,0:T(8,128)(2,1)} %param.15) | copy-start | bytes 786436
  124.2 4.1 %copy-start.23 = (s32[1,1,128]{2,1,0:T(1,128)S(1)}, s32[1,1,128]{2,1,0:T(1,128)}, u32[]{:S(2)}) copy-start(s32[1,1,128]{2,1,0:T(1,128)} %param.14) | copy-start | bytes 1540
  124.2 21.1 %all-to-all-start.4 = ((bf16[4,128,1408]{2,1,0:T(8,128)(2,1)}), bf16[4,128,1408]{2,1,0:T(8,128)(2,1)S(1)}, u32[]{:S(2)}, u32[]{:S(2)}) async-start(bf16[4,128,1408]{2,1,0:T(8,128)(2,1)} %bitcast.29), calls=%async_computation.4 | async-start | bytes 2883584 | tf_op jit(solution)/shard_map/all_to_all | solution.py:22
  145.7 4.3 %copy-start.21 = (f32[128]{0:T(128)}, f32[128]{0:T(128)S(1)}, u32[]{:S(2)}) copy-start(f32[128]{0:T(128)S(1)} %fusion.76) | copy-start | bytes 1540
  146.9 3.1 %copy-start.17 = (bf16[128,1,64]{2,0,1:T(8,128)(2,1)}, bf16[128,1,64]{2,0,1:T(8,128)(2,1)S(1)}, u32[]{:S(2)}) copy-start(bf16[128,1,64]{2,0,1:T(8,128)(2,1)S(1)} %get-tuple-element.71) | copy-start | bytes 49156
  147.0 3.1 %copy-start.19 = (bf16[128,1,64]{2,0,1:T(8,128)(2,1)}, bf16[128,1,64]{2,0,1:T(8,128)(2,1)S(1)}, u32[]{:S(2)}) copy-start(bf16[128,1,64]{2,0,1:T(8,128)(2,1)S(1)} %get-tuple-element.72) | copy-start | bytes 49156
  147.1 3.0 copy-start.4
  147.1 2.9 copy-start.6
  147.6 2.5 copy-start.22
  233.8 13.5 %copy-start.9 = (bf16[1,256,1024]{2,1,0:T(8,128)(2,1)S(1)}, bf16[1,256,1024]{2,1,0:T(8,128)(2,1)}, u32[]{:S(2)}) copy-start(bf16[1,256,1024]{2,1,0:T(8,128)(2,1)} %param.9) | copy-start | bytes 1572868
  233.8 16.4 %copy-start.3 = (bf16[512,256]{1,0:T(8,128)(2,1)S(1)}, bf16[512,256]{1,0:T(8,128)(2,1)}, u32[]{:S(2)}) copy-start(bf16[512,256]{1,0:T(8,128)(2,1)} %reduce_sum.117) | copy-start | bytes 786436
  233.8 16.4 %copy-start.13 = (bf16[8,64,256]{2,1,0:T(8,128)(2,1)S(1)}, bf16[8,64,256]{2,1,0:T(8,128)(2,1)}, u32[]{:S(2)}) copy-start(bf16[8,64,256]{2,1,0:T(8,128)(2,1)} %copy-done.12) | copy-start | bytes 786436
  233.9 8.2 %collective-permute-start.5 = (bf16[64,256]{1,0:T(8,128)(2,1)S(1)}, bf16[64,256]{1,0:T(8,128)(2,1)S(1)}, u32[]{:S(2)}, u32[]{:S(2)}) collective-permute-start(bf16[64,256]{1,0:T(8,128)(2,1)S(1)} %reduce_sum.118), channel_id=1, source_target_pairs={{0,224},{32,0},{64,32},{96,64},{128,96},{160,128},{192,160},{224,1... | collective-permute-start | bytes 98312 | tf_op jit(solution)/shard_map/ppermute | solution.py:30
  243.3 42.8 %all-to-all-start.8 = ((bf16[32,64,256]{2,1,0:T(8,128)(2,1)}), bf16[32,64,256]{2,1,0:T(8,128)(2,1)S(1)}, u32[]{:S(2)}, u32[]{:S(2)}) async-start(bf16[32,64,256]{2,1,0:T(8,128)(2,1)} %broadcast_in_dim.152), calls=%async_computation.8 | async-start | bytes 2097152 | tf_op jit(solution)/shard_map/all_to_all | solution.py:22
  247.3 15.7 %copy-start.5 = (bf16[128,8,64]{2,0,1:T(8,128)(2,1)S(1)}, bf16[128,8,64]{2,0,1:T(8,128)(2,1)}, u32[]{:S(2)}) copy-start(bf16[128,8,64]{2,0,1:T(8,128)(2,1)} %copy-done.4) | copy-start | bytes 393220
  247.3 15.7 %copy-start.7 = (bf16[128,8,64]{2,0,1:T(8,128)(2,1)S(1)}, bf16[128,8,64]{2,0,1:T(8,128)(2,1)}, u32[]{:S(2)}) copy-start(bf16[128,8,64]{2,0,1:T(8,128)(2,1)} %copy-done.6) | copy-start | bytes 393220
  247.3 15.7 %copy-start.18 = (bf16[128,1,64]{2,0,1:T(8,128)(2,1)S(1)}, bf16[128,1,64]{2,0,1:T(8,128)(2,1)}, u32[]{:S(2)}) copy-start(bf16[128,1,64]{2,0,1:T(8,128)(2,1)} %copy-done.17) | copy-start | bytes 49156
  247.3 15.7 %copy-start.20 = (bf16[128,1,64]{2,0,1:T(8,128)(2,1)S(1)}, bf16[128,1,64]{2,0,1:T(8,128)(2,1)}, u32[]{:S(2)}) copy-start(bf16[128,1,64]{2,0,1:T(8,128)(2,1)} %copy-done.19) | copy-start | bytes 49156
  247.3 40.5 %collective-permute-start.8 = (bf16[256,1024]{1,0:T(8,128)(2,1)S(1)}, bf16[256,1024]{1,0:T(8,128)(2,1)}, u32[]{:S(2)}, u32[]{:S(2)}) collective-permute-start(bf16[256,1024]{1,0:T(8,128)(2,1)S(1)} %bitcast.226), channel_id=1, source_target_pairs={{0,24},{8,0},{16,8},{24,16},{1,25},{9,1},{17,9},{25,17},{2,26},{10... | collective-permute-start | bytes 1572872 | tf_op jit(solution)/shard_map/ppermute | solution.py:137
  252.5 12.7 %collective-permute-start.12 = (bf16[256,256]{1,0:T(8,128)(2,1)}, bf16[256,256]{1,0:T(8,128)(2,1)S(1)}, u32[]{:S(2)}, u32[]{:S(2)}) collective-permute-start(bf16[256,256]{1,0:T(8,128)(2,1)} %get-tuple-element.57), channel_id=1, source_target_pairs={{3,0},{7,1},{11,2},{15,3},{19,4},{23,5},{27,6},{31,7},{0,8},{4,9},... | collective-permute-start | bytes 393224 | tf_op jit(solution)/shard_map/ppermute | solution.py:202
  254.4 13.8 %collective-permute-start.11 = (bf16[256,256]{1,0:T(8,128)(2,1)}, bf16[256,256]{1,0:T(8,128)(2,1)}, u32[]{:S(2)}, u32[]{:S(2)}) collective-permute-start(bf16[256,256]{1,0:T(8,128)(2,1)} %get-tuple-element.58), channel_id=1, source_target_pairs={{2,0},{6,1},{10,2},{14,3},{18,4},{22,5},{26,6},{30,7},{3,8},{7,9},... | collective-permute-start | bytes 393224 | tf_op jit(solution)/shard_map/ppermute | solution.py:202
  257.6 26.2 %collective-permute-start.10 = (bf16[256,256]{1,0:T(8,128)(2,1)S(1)}, bf16[256,256]{1,0:T(8,128)(2,1)}, u32[]{:S(2)}, u32[]{:S(2)}) collective-permute-start(bf16[256,256]{1,0:T(8,128)(2,1)S(1)} %get-tuple-element.59), channel_id=1, source_target_pairs={{1,0},{5,1},{9,2},{13,3},{17,4},{21,5},{25,6},{29,7},{2,8},{6,9},{... | collective-permute-start | bytes 393224 | tf_op jit(solution)/shard_map/ppermute | solution.py:202
  261.7 22.1 %collective-permute-start.9 = (bf16[256,256]{1,0:T(8,128)(2,1)S(1)}, bf16[256,256]{1,0:T(8,128)(2,1)}, u32[]{:S(2)}, u32[]{:S(2)}) collective-permute-start(bf16[256,256]{1,0:T(8,128)(2,1)S(1)} %get-tuple-element.56), channel_id=1, source_target_pairs={{0,0},{4,1},{8,2},{12,3},{16,4},{20,5},{24,6},{28,7},{1,8},{5,9},{... | collective-permute-start | bytes 393224 | tf_op jit(solution)/shard_map/ppermute | solution.py:202
  265.1 28.2 %collective-permute-start.6 = (bf16[256,1024]{1,0:T(8,128)(2,1)S(1)}, bf16[256,1024]{1,0:T(8,128)(2,1)}, u32[]{:S(2)}, u32[]{:S(2)}) collective-permute-start(bf16[256,1024]{1,0:T(8,128)(2,1)S(1)} %bitcast.227), channel_id=1, source_target_pairs={{0,8},{8,16},{16,24},{24,0},{1,9},{9,17},{17,25},{25,1},{2,10},{10... | collective-permute-start | bytes 1572872 | tf_op jit(solution)/shard_map/ppermute | solution.py:137
  268.2 37.3 %collective-permute-start.7 = (bf16[256,1024]{1,0:T(8,128)(2,1)S(1)}, bf16[256,1024]{1,0:T(8,128)(2,1)S(1)}, u32[]{:S(2)}, u32[]{:S(2)}) collective-permute-start(bf16[256,1024]{1,0:T(8,128)(2,1)S(1)} %bitcast.228), channel_id=1, source_target_pairs={{0,16},{8,24},{16,0},{24,8},{1,17},{9,25},{17,1},{25,9},{2,18},{10... | collective-permute-start | bytes 1572872 | tf_op jit(solution)/shard_map/ppermute | solution.py:137
  284.8 1.5 copy-start.1

commit v2 on v1

v2 whole, which is shorter than its diff:
```python
import math

import jax
import jax.numpy as jnp
from jax import lax
from jax.experimental import pallas as pl
from jax.experimental.pallas import tpu as pltpu
from jax.sharding import PartitionSpec as P


D = 8192
DH = 128
F = 4
T = 8
NORM_EPS = 1e-05
ROPE_BASE = 500000.0
NEG_FILL = -1e30
FT = ("fsdp", "tensor")
LOW = jnp.bfloat16
WIDE = jnp.float32
VMEM = pl.BlockSpec(memory_space=pltpu.VMEM)
GRANT = 20 << 20
ANY = pl.BlockSpec(memory_space=pl.ANY)
SMEM = pl.BlockSpec(memory_space=pltpu.SMEM)


def exchange(blocks, axis):
    return lax.all_to_all(blocks, axis, 0, 0)


def spread(value, axis, count):
    return exchange(jnp.broadcast_to(value[None], (count,) + value.shape), axis)


def to_section(value, steps):
    return lax.ppermute(value, "section", [(i, (i + steps) % 8) for i in range(8)])


def around(value, axis, count, turn):
    return lax.ppermute(value, axis, [(i, (i + turn) % count) for i in range(count)])


def column_route(turn):
    pairs = []
    for f in range(F):
        for t in range(T):
            pairs.append((f * T + t, (t // 2) * T + 2 * ((f + turn) % 4) + t % 2))
    return pairs


def mm(left, right, dims):
    return lax.dot_general(
        left, right, ((dims[:1], dims[1:]), ((), ())), preferred_element_type=WIDE
    )


def shape(dims, kind=LOW):
    return jax.ShapeDtypeStruct(dims, kind)


def call(kernel, outs, args, flops, scratch=(), far=0, grant=GRANT, out=VMEM):
    moved_bytes = sum(a.size * a.dtype.itemsize for a in args)
    return pl.pallas_call(
        kernel,
        out_shape=outs,
        in_specs=[SMEM] + [VMEM] * (len(args) - 1 - far) + [ANY] * far,
        out_specs=[out] * len(outs),
        scratch_shapes=list(scratch),
        compiler_params=pltpu.CompilerParams(vmem_limit_bytes=grant),
        cost_estimate=pl.CostEstimate(
            flops=flops, bytes_accessed=moved_bytes, transcendentals=0
        ),
    )(*args)


def code_kernel(place, *refs):
    hidden, (encoder, code, rows, weight, ready) = refs[:F], refs[F:]
    copies = [pltpu.make_async_copy(encoder, weight, ready.at[F])]
    for turn in range(F):
        row = pl.multiple_of(lax.rem(place[0] + F - turn, F) * 128, 128)
        copies.append(
            pltpu.make_async_copy(hidden[turn], rows.at[pl.ds(row, 128)], ready.at[turn])
        )
    for copy in copies:
        copy.start()
    for copy in copies:
        copy.wait()
    code[...] = mm(rows[...], weight[...], (1, 1)).astype(LOW)


def decode_kernel(place, pieces, *refs):
    columns, decoded = refs[:F], refs[F]
    y = place[1] // 2
    total = jnp.zeros((512, 256), WIDE)
    for turn in range(F):
        total = total + mm(pieces[lax.rem(y + F - turn, F)], columns[turn][...], (1, 0))
    decoded[...] = total.astype(LOW)


def feature_block(tensor_index):
    return lax.rem(tensor_index, 2) * 4 + tensor_index // 2


def project_kernel(place, *refs):
    blocks, query, pair = refs[:T], refs[T], refs[T + 1]
    sent, rows = refs[T + 2 : T + 2 + F], refs[T + 2 + F]
    for turn in range(F):
        square = jnp.zeros((128, 128), WIDE)
        source = pl.multiple_of(lax.rem(place[0] + turn, F) * 128, 128)
        for k in range(T):
            part = blocks[k][pl.ds(source, 128), :]
            lane = feature_block(lax.rem(place[1] + T - k, T)) * 256
            rows[pl.ds(128 * turn, 128), pl.ds(pl.multiple_of(lane, 256), 256)] = part
            wide = jnp.square(part.astype(WIDE))
            square = square + (wide[:, :128] + wide[:, 128:])
        square = jnp.sum(square, axis=1, keepdims=True)
        high = square.astype(LOW).astype(WIDE)
        col = lax.broadcasted_iota(jnp.int32, (128, 128), 1)
        extra = jnp.where(col == 0, high, jnp.where(col == 1, square - high, 0.0))
        sent[turn][:, 1280:] = extra.astype(LOW)

    @pl.loop(0, 4)
    def _(step):
        lanes = pl.ds(pl.multiple_of(step * 256, 256), 256)
        total = mm(rows[...], query[:, lanes], (1, 0)).astype(LOW)
        for turn in range(F):
            sent[turn][:, lanes] = total[128 * turn : 128 * (turn + 1)]

    total = mm(rows[...], pair[...], (1, 0)).astype(LOW)
    for turn in range(F):
        sent[turn][:, 1024:1280] = total[128 * turn : 128 * (turn + 1)]


def stage_weights_kernel(query, key, value, turned, query_copy, pair):
    turned[:1024, :] = query[...].T
    turned[1024:1152, :] = key[...].T
    turned[1152:, :] = value[...].T
    query_copy[...] = query[...]
    pair[:, :128] = key[...]
    pair[:, 128:] = value[...]


def stage_weights(query, key, value):
    return pl.pallas_call(
        stage_weights_kernel,
        out_shape=[shape((T, 1280, 256)), shape((2048, 1024)), shape((2048, 256))],
        grid=(T,),
        in_specs=[pl.BlockSpec((256, n), lambda k: (k, 0)) for n in (1024, 128, 128)],
        out_specs=[
            pl.BlockSpec((None, 1280, 256), lambda k: (k, 0, 0)),
            pl.BlockSpec((256, 1024), lambda k: (k, 0)),
            pl.BlockSpec((256, 256), lambda k: (k, 0)),
        ],
        name="stage_weights",
        compiler_params=pltpu.CompilerParams(vmem_limit_bytes=GRANT),
        cost_estimate=pl.CostEstimate(flops=0, bytes_accessed=10 << 20, transcendentals=0),
    )(query, key, value)


def attention_kernel(*refs):
    recv, (upstream, segment, mixed, sent) = refs[:F], refs[F : F + 4]
    plain, turned_rows, cotangent, arrived, ready = refs[F + 4 :]
    seg_row = jnp.broadcast_to(segment[...].astype(WIDE), (128, 128))
    seg_col = seg_row.T
    copy = pltpu.make_async_copy(upstream, arrived, ready.at[0])
    copy.start()
    total = recv[0][:, 1024:].astype(WIDE)
    for source in range(1, F):
        total = total + recv[source][:, 1024:].astype(WIDE)
    norm_factor = lax.rsqrt((total[:, 256:257] + total[:, 257:258]) / D + NORM_EPS)
    row = lax.broadcasted_iota(jnp.int32, (128, 128), 0)
    col = lax.broadcasted_iota(jnp.int32, (128, 128), 1)
    allowed = (seg_col == seg_row) & (col <= row)
    earlier = jnp.sum((seg_row < seg_col).astype(WIDE), axis=1, keepdims=True)
    places = row.astype(WIDE) - earlier
    lane = lax.rem(col, 64).astype(WIDE)
    angles = places * jnp.exp(lane * (-2.0 * math.log(ROPE_BASE) / DH))
    cosine = jnp.cos(angles)
    sine = jnp.sin(angles)
    signed = jnp.where(col < 64, -sine, sine)

    def turn(values, side):
        return values * cosine + pltpu.roll(values, 64, 1) * side

    factor = 1.0 / math.sqrt(DH)
    keys = total[:, :128] * norm_factor
    values = total[:, 128:256] * norm_factor
    key_rot = turn(keys, signed).astype(LOW)
    value_low = values.astype(LOW)
    heads = [(slice(128 * h, 128 * (h + 1)),) * 2 for h in range(8)]
    for rows, lanes in heads:
        queries = recv[0][:, lanes].astype(WIDE)
        for source in range(1, F):
            queries = queries + recv[source][:, lanes].astype(WIDE)
        queries = queries * norm_factor
        plain[rows, :] = queries
        turned_rows[rows, :] = turn(queries, signed).astype(LOW)

    copy.wait()
    for rows, lanes in heads:
        cotangent[rows, :] = arrived[:, lanes]
    scores = mm(turned_rows[...], key_rot, (1, 1)).reshape(8, 128, 128) * factor
    scores = jnp.where(allowed[None], scores, NEG_FILL)
    exponent = jnp.exp(scores - jnp.max(scores, axis=2, keepdims=True))
    probs = exponent / jnp.sum(exponent, axis=2, keepdims=True)
    probs_low = probs.astype(LOW).reshape(1024, 128)
    prob_grad = mm(cotangent[...], value_low, (1, 1)).reshape(8, 128, 128)
    inner = jnp.sum(probs * prob_grad, axis=2, keepdims=True)
    score_grad = (probs * (prob_grad - inner)).astype(LOW).reshape(1024, 128)
    attended = mm(probs_low, value_low, (1, 0)).astype(LOW)
    query_rot_grad = mm(score_grad, key_rot, (1, 0))
    value_grad = mm(probs_low, cotangent[...], (0, 0))
    key_grad = turn(mm(score_grad, turned_rows[...], (0, 0)) * factor, -signed)
    weight = keys * key_grad + values * value_grad
    for rows, lanes in heads:
        mixed[:, lanes] = attended[rows]
        query_grad = turn(query_rot_grad[rows] * factor, -signed)
        weight = weight + plain[rows, :] * query_grad
        sent[:, lanes] = (query_grad * norm_factor).astype(LOW)
    sent[:, 1024:1152] = (key_grad * norm_factor).astype(LOW)
    sent[:, 1152:1280] = (value_grad * norm_factor).astype(LOW)
    radial = jnp.sum(weight, axis=1, keepdims=True) * jnp.square(norm_factor) / D
    high = radial.astype(LOW).astype(WIDE)
    extra = jnp.where(col == 0, high, jnp.where(col == 1, radial - high, 0.0))
    sent[:, 1280:] = extra.astype(LOW)


def attention_stage(recv, upstream, segment_row):
    return pl.pallas_call(
        attention_kernel,
        out_shape=(
            shape((128, 1024)),
            shape((128, 1408)),
        ),
        in_specs=[VMEM] * F + [ANY, VMEM],
        out_specs=[VMEM] * 2,
        scratch_shapes=[
            pltpu.VMEM((1024, 128), WIDE),
            pltpu.VMEM((1024, 128), LOW),
            pltpu.VMEM((1024, 128), LOW),
            pltpu.VMEM((128, 1024), LOW),
            pltpu.SemaphoreType.DMA((1,)),
        ],
        name="attention_stage",
        compiler_params=pltpu.CompilerParams(vmem_limit_bytes=GRANT),
        cost_estimate=pl.CostEstimate(
            flops=14 * 8 * 128**3, bytes_accessed=3 << 20, transcendentals=8 * 128 * 128
        ),
    )(*recv, upstream, segment_row)


def share_kernel(place, *refs):
    grads, blocks, turned, out = refs[:F], refs[F : F + T], refs[F + T], refs[F + T + 1]
    rows, radial = refs[-2:]
    for turn in range(F):
        target = pl.multiple_of(lax.rem(place[0] + F - turn, F) * 128, 128)
        rows[pl.ds(target, 128), :] = grads[turn][:, :1280]
        extra = grads[turn][:, 1280:].astype(WIDE)
        radial[pl.ds(target, 128), :] = jnp.broadcast_to(
            extra[:, :1] + extra[:, 1:2], (128, 128)
        )
    for turn in range(T):
        target = lax.rem(place[1] + turn, T)
        total = mm(rows[...], turned[feature_block(target)], (1, 0))
        scale = radial[...]
        for half in range(2):
            lanes = slice(128 * half, 128 * (half + 1))
            block = blocks[(T - turn) % T][:, lanes].astype(WIDE)
            out[target, :, lanes] = (total[:, lanes] - block * scale).astype(LOW)


def code_share_kernel(place, *refs):
    parts, columns, decoded_grad, code_share = refs[0], refs[1 : 1 + F], refs[-2], refs[-1]
    total = parts[0].astype(WIDE)
    for turn in range(1, T):
        total = total + parts[turn].astype(WIDE)
    low = total.astype(LOW)
    decoded_grad[...] = low
    y = place[1] // 2
    for turn in range(F):
        code_share[lax.rem(y + F - turn, F)] = mm(low, columns[turn][...], (1, 1)).astype(LOW)


def decoder_part_kernel(place, pieces, decoded_grad, *outs):
    y = place[1] // 2
    for turn in range(F):
        outs[turn][...] = mm(
            pieces[lax.rem(y + F - turn, F)], decoded_grad[...], (0, 0)
        ).astype(LOW)


def encoder_grad_kernel(place, columns, *refs):
    hidden, encoder_grad = refs[:F], refs[F]
    for turn in range(F):
        row = pl.multiple_of(lax.rem(place[0] + F - turn, F) * 128, 128)
        part = mm(columns[pl.ds(row, 128), :], hidden[turn][...], (0, 0))
        if turn == 0:
            encoder_grad[...] = part
        else:
            encoder_grad[...] += part


def hidden_grad_kernel(place, rows, *refs):
    encoder, hidden_grad = refs[:F], refs[F]
    total = mm(rows[place[0]], encoder[0][...], (1, 0))
    for turn in range(1, F):
        part = rows[lax.rem(place[0] + F - turn, F)]
        total = total + mm(part, encoder[turn][...], (1, 0))
    hidden_grad[...] = total.astype(LOW)


def section_step(
    hidden,
    encoder_weight,
    decoder_weight,
    query_weight,
    key_weight,
    value_weight,
    segments,
    out_grad,
):
    f = lax.axis_index("fsdp")
    t = lax.axis_index("tensor")
    place = jnp.stack([f, t]).astype(jnp.int32)
    encoder = encoder_weight[0]
    decoder = decoder_weight[0]
    weights = (query_weight[0], key_weight[0], value_weight[0])

    hidden_parts = [hidden[0]]
    for turn in range(1, F):
        hidden_parts.append(around(hidden[0], "fsdp", F, turn))

    decoder_parts = []
    for turn in range(F):
        start = pl.multiple_of(lax.rem(f + turn, 4) * 256, 256)
        block = lax.dynamic_slice_in_dim(decoder, start, 256, 1)
        decoder_parts.append(lax.ppermute(block, FT, column_route(turn)))

    small = 2 * 512 * 1024 * 256
    (code_part,) = call(
        code_kernel,
        [shape((512, 256))],
        [place, *hidden_parts, encoder],
        small,
        [
            pltpu.VMEM((512, 1024), LOW),
            pltpu.VMEM((256, 1024), LOW),
            pltpu.SemaphoreType.DMA((F + 1,)),
        ],
        far=F + 1,
        grant=None,
    )
    came = exchange(code_part.reshape(T, 64, 256), "tensor")
    code_piece = jnp.sum(came.astype(WIDE), axis=0).astype(LOW)
    code_moved = to_section(code_piece, 1)
    pieces = spread(code_moved, FT, F * T).reshape(F, 512, 256)

    (decoded,) = call(
        decode_kernel, [shape((512, 256))], [place, pieces, *decoder_parts], small
    )
    blocks = [decoded]
    for turn in range(1, T):
        blocks.append(around(decoded, "tensor", T, turn))

    encoder, decoded = lax.optimization_barrier((encoder, decoded))
    encoder_parts = [encoder]
    for turn in range(1, F):
        encoder_parts.append(around(encoder, "fsdp", F, turn))

    turned, query, pair = stage_weights(*weights)
    sent = call(
        project_kernel,
        [shape((128, 1408))] * F,
        [place, *blocks, query, pair],
        10 * small,
        [pltpu.VMEM((512, 2048), LOW)],
    )
    came = [sent[0]]
    for turn in range(1, F):
        came.append(around(sent[turn], "fsdp", F, turn))
    mixed, sent = attention_stage(came, out_grad[0], segments[0])
    grads = [sent]
    for turn in range(1, F):
        grads.append(around(sent, "fsdp", F, turn))

    (share,) = call(
        share_kernel,
        [shape((T, 512, 256))],
        [place, *grads, *blocks, turned],
        10 * small,
        [pltpu.VMEM((512, 1280), LOW), pltpu.VMEM((512, 128), WIDE)],
    )
    parts = exchange(share, "tensor")
    decoded_grad, code_share = call(
        code_share_kernel,
        [shape((512, 256)), shape((F, 512, 256))],
        [place, parts, *decoder_parts],
        small,
    )
    came = exchange(code_share.reshape(F * T, 64, 256), FT)
    grad_piece = jnp.sum(came.astype(WIDE), axis=0).astype(LOW)
    grad_moved = to_section(grad_piece, -1)

    decoder_blocks = call(
        decoder_part_kernel,
        [shape((256, 256))] * F,
        [place, pieces, decoded_grad],
        small,
    )
    came = []
    for turn in range(F):
        back = [(target, source) for source, target in column_route(turn)]
        came.append(lax.ppermute(decoder_blocks[turn], FT, back))
    came = jnp.stack(came)
    decoder_grad = jnp.concatenate(
        [
            lax.dynamic_index_in_dim(came, (c + 4 - f) % 4, 0, keepdims=False)
            for c in range(4)
        ],
        axis=1,
    ).astype(WIDE)

    code_grad = spread(grad_moved, "tensor", T).reshape(512, 256)
    grad_rows = exchange(code_grad.reshape(F, 128, 256), "fsdp")
    (encoder_grad,) = call(
        encoder_grad_kernel,
        [shape((256, 1024), WIDE)],
        [place, code_grad, *hidden_parts],
        small,
    )
    (hidden_grad,) = call(
        hidden_grad_kernel,
        [shape((128, 1024))],
        [place, grad_rows, *encoder_parts],
        small,
    )
    return (mixed[None], hidden_grad[None], encoder_grad[None], decoder_grad[None])


def solution(mesh):
    placed = P("section", "fsdp", "tensor")
    return jax.shard_map(
        section_step,
        mesh=mesh,
        in_specs=(placed,) * 6 + (P("section", "fsdp", None), placed),
        out_specs=(placed,) * 4,
        check_vma=False,
    )
```

time: 311 us -> 275 us (0.88)
  blocking collectives: 100 us -> 63 us
  Pallas kernels: 0 us -> 24 us
  matrix products: 21.7 us -> 0 us
  local copies, waits for them, and re-layouts: 16.2 us -> 4.94 us
  waiting for transfers between devices: 82.1 us -> 92.8 us
  starting transfers between devices: 75.4 us -> 82.1 us
  other arithmetic: 9.19 us -> 4.18 us
    ppermute x11 -> x27, waiting for transfers between devices: 33.5 us -> 85.1 us  [the longest x19 54.8 us: around(): lax.ppermute(value, axis, [(i, (i + turn) % count) for i in range(count)])]
    all_to_all x4 -> x3, waiting for transfers between devices: 42.2 us -> 1.33 us  [exchange(): return lax.all_to_all(blocks, axis, 0, 0)]
    all_to_all x5 -> x3, blocking collectives: 100 us -> 63 us  [exchange(): return lax.all_to_all(blocks, axis, 0, 0)]
    pallas_call x0 -> x10, Pallas kernels: none -> 24 us  [the longest x8 19.8 us: call(): pl.pallas_call(kernel, out_shape=outs, in_specs=[SMEM] + [VMEM] * (len(ar...]
    dot_general x16 -> x0, matrix products: 21.3 us -> none  [the longest x11 18.5 us: dot(): lax.dot_general(left, right, (((left_dim,), (right_dim,)), ((), ())), pre...]
    ppermute x11 -> x27, starting transfers between devices: 46.6 us -> 60.4 us  [the longest x19 42.4 us: around(): lax.ppermute(value, axis, [(i, (i + turn) % count) for i in range(count)])]
    all_to_all x4 -> x3, starting transfers between devices: 19.9 us -> 12.6 us  [exchange(): return lax.all_to_all(blocks, axis, 0, 0)]
    broadcast_in_dim x5 -> x2, local copies, waits for them, and re-layouts: 4.96 us -> 1.81 us  [spread(): return exchange(jnp.broadcast_to(value[None], (count,) + value.shape), axis)]
  transfers between devices with their start and end apart: 17 -> 32, of which waited for: 8 -> 17; matrix products, arithmetic and copies ran while one was open for 4% -> 1% of each run, Pallas kernels for 0% -> 2%
where the time goes in v2:
time: 275 us; the launch traced here: 272 us
  waiting for transfers between devices  92.8 us (34%)
  starting transfers between devices  82.1 us (30%)
  blocking collectives  63 us (23%)
  Pallas kernels  24 us (9%)
  local copies, waits for them, and re-layouts  4.94 us (2%)
  other arithmetic  4.18 us (2%)
    all_to_all x3, blocking collectives, exchange(): return lax.all_to_all(blocks, axis, 0, 0)  63 us
    ppermute x19, waiting for transfers between devices, around(): lax.ppermute(value, axis, [(i, (i + turn) % count) for i in range(count)])  54.8 us
    ppermute x19, starting transfers between devices, around(): lax.ppermute(value, axis, [(i, (i + turn) % count) for i in range(count)])  42.4 us
    ppermute x4, waiting for transfers between devices, section_step(): decoder_parts.append(lax.ppermute(block, FT, column_route(turn)))  20.4 us
    pallas_call x8, Pallas kernels, call(): pl.pallas_call(kernel, out_shape=outs, in_specs=[SMEM] + [VMEM] * (len(ar...  19.8 us
    all_to_all x3, starting transfers between devices, exchange(): return lax.all_to_all(blocks, axis, 0, 0)  12.6 us
    ppermute x4, starting transfers between devices, section_step(): decoder_parts.append(lax.ppermute(block, FT, column_route(turn)))  10.4 us
    ppermute x4, waiting for transfers between devices, section_step(): came.append(lax.ppermute(decoder_blocks[turn], FT, back))  9.83 us
  transfers between devices with their start and end apart: 32, of which 17 were waited for; matrix products, arithmetic and copies ran while one was open for 1% of the time, Pallas kernels for 2%

profile of v2, /device:TPU:1, one launch (start us, length us, event | category | flops | bytes accessed | tf_op | source)
XLA Modules:
  0.0 271.9 jit_solution(8370437248571828627)
XLA Ops:
  0.6 2.1 collective-permute-start
  2.7 2.5 collective-permute-start.1
  5.2 1.2 collective-permute-start.2
  8.0 8.8 %collective-permute-done.1.refs_2_ = bf16[128,1024]{1,0:T(8,128)(2,1)S(1)} collective-permute-done((bf16[128,1024]{1,0:T(8,128)(2,1)}, bf16[128,1024]{1,0:T(8,128)(2,1)S(1)}, u32[]{:S(2)}, u32[]{:S(2)}) %collective-permute-start.1) | collective-permute-done | bytes 262176 | tf_op jit(solution)/shard_map/ppermute | solution.py:40
  17.5 3.4 %shard_map.111 = bf16[512,256]{1,0:T(8,128)(2,1)} custom-call(s32[2]{0:T(128)} %pad_add_fusion.place, bf16[128,1024]{1,0:T(8,128)(2,1)} %bitcast.41, bf16[128,1024]{1,0:T(8,128)(2,1)} %copy-done.3, bf16[128,1024]{1,0:T(8,128)(2,1)} %copy-done.5, bf16[128,1024]{1,0:T(8,128)(2,1)} %copy-done.7, bf16[256,1024]{1,0:T(8,128)(2,1)} %bitcast.32), custom_call_target="tpu_custom_call" | custom-call | flops 268435456 | bytes 1572872 | tf_op jit(solution)/shard_map/pallas_call | solution.py:63
  20.9 11.7 %all_to_all.30 = bf16[8,64,256]{2,1,0:T(8,128)(2,1)S(1)} all-to-all(bf16[8,64,256]{2,1,0:T(8,128)(2,1)} %bitcast.48), channel_id=1, replica_groups=mesh['section'=8,'fsdp'=4,'tensor'=8] {'tensor'}, dimensions={0} | all-to-all | bytes 524288 | tf_op jit(solution)/shard_map/all_to_all | solution.py:28
  32.6 5.9 %collective-permute-start.3 = (bf16[64,256]{1,0:T(8,128)(2,1)S(1)}, bf16[64,256]{1,0:T(8,128)(2,1)S(1)}, u32[]{:S(2)}, u32[]{:S(2)}) collective-permute-start(bf16[64,256]{1,0:T(8,128)(2,1)S(1)} %reduce_sum.24), channel_id=1, source_target_pairs={{0,32},{32,64},{64,96},{96,128},{128,160},{160,192},{192,224},{224... | collective-permute-start | bytes 98312 | tf_op jit(solution)/shard_map/ppermute | solution.py:36
  40.7 4.9 %all-to-all-start.1 = ((bf16[32,64,256]{2,1,0:T(8,128)(2,1)}), bf16[32,64,256]{2,1,0:T(8,128)(2,1)S(1)}, u32[]{:S(2)}, u32[]{:S(2)}) async-start(bf16[32,64,256]{2,1,0:T(8,128)(2,1)} %broadcast_in_dim.10), calls=%async_computation.1 | async-start | bytes 2097152 | tf_op jit(solution)/shard_map/all_to_all | solution.py:28
  46.3 3.7 %collective-permute-start.5 = (bf16[256,256]{1,0:T(8,128)(2,1)S(1)}, bf16[256,256]{1,0:T(8,128)(2,1)S(1)}, u32[]{:S(2)}, u32[]{:S(2)}) collective-permute-start(bf16[256,256]{1,0:T(8,128)(2,1)S(1)} %get-tuple-element.41), channel_id=1, source_target_pairs={{0,2},{1,3},{2,10},{3,11},{4,18},{5,19},{6,26},{7,27},{8,4},{9,5},... | collective-permute-start | bytes 393224 | tf_op jit(solution)/shard_map/ppermute | solution.py:337
  50.1 4.2 %collective-permute-start.6 = (bf16[256,256]{1,0:T(8,128)(2,1)S(1)}, bf16[256,256]{1,0:T(8,128)(2,1)S(1)}, u32[]{:S(2)}, u32[]{:S(2)}) collective-permute-start(bf16[256,256]{1,0:T(8,128)(2,1)S(1)} %get-tuple-element.43), channel_id=1, source_target_pairs={{0,4},{1,5},{2,12},{3,13},{4,20},{5,21},{6,28},{7,29},{8,6},{9,7},... | collective-permute-start | bytes 393224 | tf_op jit(solution)/shard_map/ppermute | solution.py:337
  54.3 1.8 collective-permute-start.7
  56.1 20.4 %collective-permute-done.5.refs_1_.refs_2_ = bf16[256,256]{1,0:T(8,128)(2,1)S(1)} collective-permute-done((bf16[256,256]{1,0:T(8,128)(2,1)S(1)}, bf16[256,256]{1,0:T(8,128)(2,1)S(1)}, u32[]{:S(2)}, u32[]{:S(2)}) %collective-permute-start.5) | collective-permute-done | bytes 131104 | tf_op jit(solution)/shard_map/ppermute | solution.py:337
  77.5 5.1 %collective-permute-start.10 = (bf16[512,256]{1,0:T(8,128)(2,1)S(1)}, bf16[512,256]{1,0:T(8,128)(2,1)S(1)}, u32[]{:S(2)}, u32[]{:S(2)}) collective-permute-start(bf16[512,256]{1,0:T(8,128)(2,1)S(1)} %shard_map.112.refs_0_.refs_4_), channel_id=1, source_target_pairs={{0,3},{1,4},{2,5},{3,6},{4,7},{5,0},{6,1},{7,2},{8,11},{9,12},{10,... | collective-permute-start | bytes 786440 | tf_op jit(solution)/shard_map/ppermute | solution.py:40
  82.5 3.4 %collective-permute-start.11 = (bf16[512,256]{1,0:T(8,128)(2,1)S(1)}, bf16[512,256]{1,0:T(8,128)(2,1)S(1)}, u32[]{:S(2)}, u32[]{:S(2)}) collective-permute-start(bf16[512,256]{1,0:T(8,128)(2,1)S(1)} %shard_map.112.refs_0_.refs_4_), channel_id=1, source_target_pairs={{0,4},{1,5},{2,6},{3,7},{4,0},{5,1},{6,2},{7,3},{8,12},{9,13},{10,... | collective-permute-start | bytes 786440 | tf_op jit(solution)/shard_map/ppermute | solution.py:40
  85.9 3.8 %collective-permute-start.12 = (bf16[512,256]{1,0:T(8,128)(2,1)S(1)}, bf16[512,256]{1,0:T(8,128)(2,1)S(1)}, u32[]{:S(2)}, u32[]{:S(2)}) collective-permute-start(bf16[512,256]{1,0:T(8,128)(2,1)S(1)} %shard_map.112.refs_0_.refs_4_), channel_id=1, source_target_pairs={{0,5},{1,6},{2,7},{3,0},{4,1},{5,2},{6,3},{7,4},{8,13},{9,14},{10,... | collective-permute-start | bytes 786440 | tf_op jit(solution)/shard_map/ppermute | solution.py:40
  90.0 2.3 collective-permute-done.10.refs_3_.refs_7_
  92.3 5.1 %collective-permute-done.11.refs_4_.refs_8_ = bf16[512,256]{1,0:T(8,128)(2,1)S(1)} collective-permute-done((bf16[512,256]{1,0:T(8,128)(2,1)S(1)}, bf16[512,256]{1,0:T(8,128)(2,1)S(1)}, u32[]{:S(2)}, u32[]{:S(2)}) %collective-permute-start.11) | collective-permute-done | bytes 262176 | tf_op jit(solution)/shard_map/ppermute | solution.py:40
  97.4 7.2 %collective-permute-start.9 = (bf16[512,256]{1,0:T(8,128)(2,1)S(1)}, bf16[512,256]{1,0:T(8,128)(2,1)S(1)}, u32[]{:S(2)}, u32[]{:S(2)}) collective-permute-start(bf16[512,256]{1,0:T(8,128)(2,1)S(1)} %shard_map.112.refs_0_.refs_4_), channel_id=1, source_target_pairs={{0,2},{1,3},{2,4},{3,5},{4,6},{5,7},{6,0},{7,1},{8,10},{9,11},{10,... | collective-permute-start | bytes 786440 | tf_op jit(solution)/shard_map/ppermute | solution.py:40
  104.6 2.2 copy-done
  106.8 1.9 stage_weights.1
  108.7 1.6 collective-permute-done.13.refs_6_.refs_10_
  110.3 4.3 %collective-permute-done.9.refs_2_.refs_6_ = bf16[512,256]{1,0:T(8,128)(2,1)S(1)} collective-permute-done((bf16[512,256]{1,0:T(8,128)(2,1)S(1)}, bf16[512,256]{1,0:T(8,128)(2,1)S(1)}, u32[]{:S(2)}, u32[]{:S(2)}) %collective-permute-start.9) | collective-permute-done | bytes 262176 | tf_op jit(solution)/shard_map/ppermute | solution.py:40
  114.7 4.7 %shard_map.113 = (bf16[128,1408]{1,0:T(8,128)(2,1)S(1)}, bf16[128,1408]{1,0:T(8,128)(2,1)S(1)}, bf16[128,1408]{1,0:T(8,128)(2,1)S(1)}, bf16[128,1408]{1,0:T(8,128)(2,1)S(1)}) custom-call(s32[2]{0:T(128)S(1)} %copy-done.12, bf16[512,256]{1,0:T(8,128)(2,1)S(1)} %shard_map.112.refs_0_.refs_4_, bf16[512,256]{1,0:T(8,128)(2,1)S(1)} %collective-permute-done.8.refs_1_.refs_5_, ...), custom_call_target="tpu_custom_call" | custom-call | flops 2684354560 | bytes 7340040 | tf_op jit(solution)/shard_map/pallas_call | solution.py:63
  120.4 2.2 collective-permute-start.16
  122.7 1.5 collective-permute-start.17
  124.2 5.6 %collective-permute-done.15.refs_1_ = bf16[128,1408]{1,0:T(8,128)(2,1)S(1)} collective-permute-done((bf16[128,1408]{1,0:T(8,128)(2,1)S(1)}, bf16[128,1408]{1,0:T(8,128)(2,1)S(1)}, u32[]{:S(2)}, u32[]{:S(2)}) %collective-permute-start.15) | collective-permute-done | bytes 360480 | tf_op jit(solution)/shard_map/ppermute | solution.py:40
  129.7 8.5 %collective-permute-done.16.refs_2_ = bf16[128,1408]{1,0:T(8,128)(2,1)S(1)} collective-permute-done((bf16[128,1408]{1,0:T(8,128)(2,1)S(1)}, bf16[128,1408]{1,0:T(8,128)(2,1)S(1)}, u32[]{:S(2)}, u32[]{:S(2)}) %collective-permute-start.16) | collective-permute-done | bytes 360480 | tf_op jit(solution)/shard_map/ppermute | solution.py:40
  138.3 2.3 attention_stage.1
  140.6 2.0 collective-permute-start.18
  142.6 2.6 collective-permute-start.19
  145.3 6.4 %collective-permute-done.18.refs_1_ = bf16[128,1408]{1,0:T(8,128)(2,1)S(1)} collective-permute-done((bf16[128,1408]{1,0:T(8,128)(2,1)S(1)}, bf16[128,1408]{1,0:T(8,128)(2,1)S(1)}, u32[]{:S(2)}, u32[]{:S(2)}) %collective-permute-start.18) | collective-permute-done | bytes 360480 | tf_op jit(solution)/shard_map/ppermute | solution.py:40
  151.8 9.2 %collective-permute-done.19.refs_2_ = bf16[128,1408]{1,0:T(8,128)(2,1)S(1)} collective-permute-done((bf16[128,1408]{1,0:T(8,128)(2,1)S(1)}, bf16[128,1408]{1,0:T(8,128)(2,1)S(1)}, u32[]{:S(2)}, u32[]{:S(2)}) %collective-permute-start.19) | collective-permute-done | bytes 360480 | tf_op jit(solution)/shard_map/ppermute | solution.py:40
  161.0 3.7 %shard_map.114 = bf16[8,512,256]{2,1,0:T(8,128)(2,1)S(1)} custom-call(s32[2]{0:T(128)S(1)} %copy-done.12, bf16[128,1408]{1,0:T(8,128)(2,1)S(1)} %get-tuple-element.27.refs_0_, bf16[128,1408]{1,0:T(8,128)(2,1)S(1)} %collective-permute-done.18.refs_1_, bf16[128,1408]{1,0:T(8,128)(2,1)S(1)} %collective-permute-done.19.refs_2_, ...), custom_call_target="tpu_custom_call" | custom-call | flops 2684354560 | bytes 8781832 | tf_op jit(solution)/shard_map/pallas_call | solution.py:63
  164.7 29.3 %all_to_all.31.refs_0_ = bf16[8,512,256]{2,1,0:T(8,128)(2,1)S(1)} all-to-all(bf16[8,512,256]{2,1,0:T(8,128)(2,1)S(1)} %shard_map.114), channel_id=1, replica_groups=mesh['section'=8,'fsdp'=4,'tensor'=8] {'tensor'}, dimensions={0} | all-to-all | bytes 4194304 | tf_op jit(solution)/shard_map/all_to_all | solution.py:28
  195.1 22.1 %all_to_all.32 = bf16[32,64,256]{2,1,0:T(8,128)(2,1)} all-to-all(bf16[32,64,256]{2,1,0:T(8,128)(2,1)S(1)} %bitcast.37), channel_id=1, replica_groups=mesh['section'=8,'fsdp'=4,'tensor'=8] {'fsdp','tensor'}, dimensions={0} | all-to-all | bytes 2097152 | tf_op jit(solution)/shard_map/all_to_all | solution.py:28
  217.2 1.5 reduce_sum.25
  218.7 3.2 %collective-permute-start.21 = (bf16[64,256]{1,0:T(8,128)(2,1)S(1)}, bf16[64,256]{1,0:T(8,128)(2,1)S(1)}, u32[]{:S(2)}, u32[]{:S(2)}) collective-permute-start(bf16[64,256]{1,0:T(8,128)(2,1)S(1)} %reduce_sum.25), channel_id=1, source_target_pairs={{0,224},{32,0},{64,32},{96,64},{128,96},{160,128},{192,160},{224,1... | collective-permute-start | bytes 98312 | tf_op jit(solution)/shard_map/ppermute | solution.py:36
  221.8 5.4 %collective-permute-done.21 = bf16[64,256]{1,0:T(8,128)(2,1)S(1)} collective-permute-done((bf16[64,256]{1,0:T(8,128)(2,1)S(1)}, bf16[64,256]{1,0:T(8,128)(2,1)S(1)}, u32[]{:S(2)}, u32[]{:S(2)}) %collective-permute-start.21) | collective-permute-done | bytes 32800 | tf_op jit(solution)/shard_map/ppermute | solution.py:36
  227.9 4.0 %all-to-all-start.4 = ((bf16[8,64,256]{2,1,0:T(8,128)(2,1)}), bf16[8,64,256]{2,1,0:T(8,128)(2,1)}, u32[]{:S(2)}, u32[]{:S(2)}) async-start(bf16[8,64,256]{2,1,0:T(8,128)(2,1)} %broadcast_in_dim.24), calls=%async_computation.4 | async-start | bytes 524288 | tf_op jit(solution)/shard_map/all_to_all | solution.py:28
  233.7 6.3 %collective-permute-start.26 = (bf16[256,256]{1,0:T(8,128)(2,1)S(1)}, bf16[256,256]{1,0:T(8,128)(2,1)S(1)}, u32[]{:S(2)}, u32[]{:S(2)}) collective-permute-start(bf16[256,256]{1,0:T(8,128)(2,1)S(1)} %get-tuple-element.33), channel_id=1, source_target_pairs={{2,0},{3,1},{10,2},{11,3},{18,4},{19,5},{26,6},{27,7},{4,8},{5,9},... | collective-permute-start | bytes 393224 | tf_op jit(solution)/shard_map/ppermute | solution.py:413
  241.5 2.7 collective-permute-start.23
  244.1 9.8 %collective-permute-done.26 = bf16[256,256]{1,0:T(8,128)(2,1)S(1)} collective-permute-done((bf16[256,256]{1,0:T(8,128)(2,1)S(1)}, bf16[256,256]{1,0:T(8,128)(2,1)S(1)}, u32[]{:S(2)}, u32[]{:S(2)}) %collective-permute-start.26) | collective-permute-done | bytes 131104 | tf_op jit(solution)/shard_map/ppermute | solution.py:413
  254.0 4.0 %collective-permute-start.24 = (bf16[256,1024]{1,0:T(8,128)(2,1)S(1)}, bf16[256,1024]{1,0:T(8,128)(2,1)}, u32[]{:S(2)}, u32[]{:S(2)}) collective-permute-start(bf16[256,1024]{1,0:T(8,128)(2,1)S(1)} %bitcast.35), channel_id=1, source_target_pairs={{0,24},{8,0},{16,8},{24,16},{1,25},{9,1},{17,9},{25,17},{2,26},{10... | collective-permute-start | bytes 1572872 | tf_op jit(solution)/shard_map/ppermute | solution.py:40
  259.0 3.7 %all-to-all-start.5 = ((bf16[4,128,256]{2,1,0:T(8,128)(2,1)}), bf16[4,128,256]{2,1,0:T(8,128)(2,1)S(1)}, u32[]{:S(2)}, u32[]{:S(2)}) async-start(bf16[4,128,256]{2,1,0:T(8,128)(2,1)} %bitcast.17), calls=%async_computation.5 | async-start | bytes 524288 | tf_op jit(solution)/shard_map/all_to_all | solution.py:28
  263.8 2.7 shard_map.117
  266.5 1.9 collective-permute-done.23.refs_2_
  268.3 1.3 all-to-all-done.5.rows
  269.7 2.2 shard_map.116
  (68 shorter events, 15.0 us)
Async XLA Ops:
  0.6 44.9 %copy-start.14 = (bf16[1,256,1024]{2,1,0:T(8,128)(2,1)S(1)}, bf16[1,256,1024]{2,1,0:T(8,128)(2,1)}, u32[]{:S(2)}) copy-start(bf16[1,256,1024]{2,1,0:T(8,128)(2,1)} %param.10) | copy-start | bytes 1572868
  0.6 7.3 %collective-permute-start = (bf16[128,1024]{1,0:T(8,128)(2,1)}, bf16[128,1024]{1,0:T(8,128)(2,1)S(1)}, u32[]{:S(2)}, u32[]{:S(2)}) collective-permute-start(bf16[128,1024]{1,0:T(8,128)(2,1)} %bitcast.38), channel_id=1, source_target_pairs={{0,8},{8,16},{16,24},{24,0},{1,9},{9,17},{17,25},{25,1},{2,10},{10... | collective-permute-start | bytes 786440 | tf_op jit(solution)/shard_map/ppermute | solution.py:40
  2.7 14.0 %collective-permute-start.1 = (bf16[128,1024]{1,0:T(8,128)(2,1)}, bf16[128,1024]{1,0:T(8,128)(2,1)S(1)}, u32[]{:S(2)}, u32[]{:S(2)}) collective-permute-start(bf16[128,1024]{1,0:T(8,128)(2,1)} %bitcast.39), channel_id=1, source_target_pairs={{0,16},{8,24},{16,0},{24,8},{1,17},{9,25},{17,1},{25,9},{2,18},{10... | collective-permute-start | bytes 786440 | tf_op jit(solution)/shard_map/ppermute | solution.py:40
  5.2 11.6 %collective-permute-start.2 = (bf16[128,1024]{1,0:T(8,128)(2,1)}, bf16[128,1024]{1,0:T(8,128)(2,1)S(1)}, u32[]{:S(2)}, u32[]{:S(2)}) collective-permute-start(bf16[128,1024]{1,0:T(8,128)(2,1)} %bitcast.40), channel_id=1, source_target_pairs={{0,24},{8,0},{16,8},{24,16},{1,25},{9,1},{17,9},{25,17},{2,26},{10... | collective-permute-start | bytes 786440 | tf_op jit(solution)/shard_map/ppermute | solution.py:40
  7.0 69.5 %copy-start.12 = (s32[2]{0:T(128)S(1)}, s32[2]{0:T(128)}, u32[]{:S(2)}) copy-start(s32[2]{0:T(128)} %pad_add_fusion.place) | copy-start | bytes 28
  8.0 8.8 %copy-start.3 = (bf16[128,1024]{1,0:T(8,128)(2,1)}, bf16[128,1024]{1,0:T(8,128)(2,1)S(1)}, u32[]{:S(2)}) copy-start(bf16[128,1024]{1,0:T(8,128)(2,1)S(1)} %collective-permute-done.refs_1_) | copy-start | bytes 786436
  16.8 0.7 copy-start.5
  16.8 0.8 copy-start.7
  17.5 87.0 %copy-start.9 = (bf16[1,2048,128]{2,1,0:T(8,128)(2,1)S(1)}, bf16[1,2048,128]{2,1,0:T(8,128)(2,1)}, u32[]{:S(2)}) copy-start(bf16[1,2048,128]{2,1,0:T(8,128)(2,1)} %param.12) | copy-start | bytes 1572868
  17.5 87.0 %copy-start.10 = (bf16[1,2048,128]{2,1,0:T(8,128)(2,1)S(1)}, bf16[1,2048,128]{2,1,0:T(8,128)(2,1)}, u32[]{:S(2)}) copy-start(bf16[1,2048,128]{2,1,0:T(8,128)(2,1)} %param.13) | copy-start | bytes 1572868
  32.6 6.9 %collective-permute-start.3 = (bf16[64,256]{1,0:T(8,128)(2,1)S(1)}, bf16[64,256]{1,0:T(8,128)(2,1)S(1)}, u32[]{:S(2)}, u32[]{:S(2)}) collective-permute-start(bf16[64,256]{1,0:T(8,128)(2,1)S(1)} %reduce_sum.24), channel_id=1, source_target_pairs={{0,32},{32,64},{64,96},{96,128},{128,160},{160,192},{192,224},{224... | collective-permute-start | bytes 98312 | tf_op jit(solution)/shard_map/ppermute | solution.py:36
  40.7 35.8 %all-to-all-start.1 = ((bf16[32,64,256]{2,1,0:T(8,128)(2,1)}), bf16[32,64,256]{2,1,0:T(8,128)(2,1)S(1)}, u32[]{:S(2)}, u32[]{:S(2)}) async-start(bf16[32,64,256]{2,1,0:T(8,128)(2,1)} %broadcast_in_dim.10), calls=%async_computation.1 | async-start | bytes 2097152 | tf_op jit(solution)/shard_map/all_to_all | solution.py:28
  45.7 10.4 %collective-permute-start.4 = (bf16[256,256]{1,0:T(8,128)(2,1)S(1)}, bf16[256,256]{1,0:T(8,128)(2,1)S(1)}, u32[]{:S(2)}, u32[]{:S(2)}) collective-permute-start(bf16[256,256]{1,0:T(8,128)(2,1)S(1)} %get-tuple-element.42), channel_id=1, source_target_pairs={{0,0},{1,1},{2,8},{3,9},{4,16},{5,17},{6,24},{7,25},{8,2},{9,3},{1... | collective-permute-start | bytes 393224 | tf_op jit(solution)/shard_map/ppermute | solution.py:337
  46.3 30.1 %collective-permute-start.5 = (bf16[256,256]{1,0:T(8,128)(2,1)S(1)}, bf16[256,256]{1,0:T(8,128)(2,1)S(1)}, u32[]{:S(2)}, u32[]{:S(2)}) collective-permute-start(bf16[256,256]{1,0:T(8,128)(2,1)S(1)} %get-tuple-element.41), channel_id=1, source_target_pairs={{0,2},{1,3},{2,10},{3,11},{4,18},{5,19},{6,26},{7,27},{8,4},{9,5},... | collective-permute-start | bytes 393224 | tf_op jit(solution)/shard_map/ppermute | solution.py:337
  50.1 26.4 %collective-permute-start.6 = (bf16[256,256]{1,0:T(8,128)(2,1)S(1)}, bf16[256,256]{1,0:T(8,128)(2,1)S(1)}, u32[]{:S(2)}, u32[]{:S(2)}) collective-permute-start(bf16[256,256]{1,0:T(8,128)(2,1)S(1)} %get-tuple-element.43), channel_id=1, source_target_pairs={{0,4},{1,5},{2,12},{3,13},{4,20},{5,21},{6,28},{7,29},{8,6},{9,7},... | collective-permute-start | bytes 393224 | tf_op jit(solution)/shard_map/ppermute | solution.py:337
  54.3 22.2 %collective-permute-start.7 = (bf16[256,256]{1,0:T(8,128)(2,1)S(1)}, bf16[256,256]{1,0:T(8,128)(2,1)S(1)}, u32[]{:S(2)}, u32[]{:S(2)}) collective-permute-start(bf16[256,256]{1,0:T(8,128)(2,1)S(1)} %get-tuple-element.40), channel_id=1, source_target_pairs={{0,6},{1,7},{2,14},{3,15},{4,22},{5,23},{6,30},{7,31},{8,0},{9,1},... | collective-permute-start | bytes 393224 | tf_op jit(solution)/shard_map/ppermute | solution.py:337
  77.5 14.9 %collective-permute-start.10 = (bf16[512,256]{1,0:T(8,128)(2,1)S(1)}, bf16[512,256]{1,0:T(8,128)(2,1)S(1)}, u32[]{:S(2)}, u32[]{:S(2)}) collective-permute-start(bf16[512,256]{1,0:T(8,128)(2,1)S(1)} %shard_map.112.refs_0_.refs_4_), channel_id=1, source_target_pairs={{0,3},{1,4},{2,5},{3,6},{4,7},{5,0},{6,1},{7,2},{8,11},{9,12},{10,... | collective-permute-start | bytes 786440 | tf_op jit(solution)/shard_map/ppermute | solution.py:40
  82.5 14.9 %collective-permute-start.11 = (bf16[512,256]{1,0:T(8,128)(2,1)S(1)}, bf16[512,256]{1,0:T(8,128)(2,1)S(1)}, u32[]{:S(2)}, u32[]{:S(2)}) collective-permute-start(bf16[512,256]{1,0:T(8,128)(2,1)S(1)} %shard_map.112.refs_0_.refs_4_), channel_id=1, source_target_pairs={{0,4},{1,5},{2,6},{3,7},{4,0},{5,1},{6,2},{7,3},{8,12},{9,13},{10,... | collective-permute-start | bytes 786440 | tf_op jit(solution)/shard_map/ppermute | solution.py:40
  85.9 22.8 %collective-permute-start.12 = (bf16[512,256]{1,0:T(8,128)(2,1)S(1)}, bf16[512,256]{1,0:T(8,128)(2,1)S(1)}, u32[]{:S(2)}, u32[]{:S(2)}) collective-permute-start(bf16[512,256]{1,0:T(8,128)(2,1)S(1)} %shard_map.112.refs_0_.refs_4_), channel_id=1, source_target_pairs={{0,5},{1,6},{2,7},{3,0},{4,1},{5,2},{6,3},{7,4},{8,13},{9,14},{10,... | collective-permute-start | bytes 786440 | tf_op jit(solution)/shard_map/ppermute | solution.py:40
  89.7 20.6 %collective-permute-start.13 = (bf16[512,256]{1,0:T(8,128)(2,1)S(1)}, bf16[512,256]{1,0:T(8,128)(2,1)S(1)}, u32[]{:S(2)}, u32[]{:S(2)}) collective-permute-start(bf16[512,256]{1,0:T(8,128)(2,1)S(1)} %shard_map.112.refs_0_.refs_4_), channel_id=1, source_target_pairs={{0,6},{1,7},{2,0},{3,1},{4,2},{5,3},{6,4},{7,5},{8,14},{9,15},{10,... | collective-permute-start | bytes 786440 | tf_op jit(solution)/shard_map/ppermute | solution.py:40
  89.7 20.6 %collective-permute-start.14 = (bf16[512,256]{1,0:T(8,128)(2,1)S(1)}, bf16[512,256]{1,0:T(8,128)(2,1)S(1)}, u32[]{:S(2)}, u32[]{:S(2)}) collective-permute-start(bf16[512,256]{1,0:T(8,128)(2,1)S(1)} %shard_map.112.refs_0_.refs_4_), channel_id=1, source_target_pairs={{0,7},{1,0},{2,1},{3,2},{4,3},{5,4},{6,5},{7,6},{8,15},{9,8},{10,9... | collective-permute-start | bytes 786440 | tf_op jit(solution)/shard_map/ppermute | solution.py:40
  92.3 18.0 %collective-permute-start.8 = (bf16[512,256]{1,0:T(8,128)(2,1)S(1)}, bf16[512,256]{1,0:T(8,128)(2,1)S(1)}, u32[]{:S(2)}, u32[]{:S(2)}) collective-permute-start(bf16[512,256]{1,0:T(8,128)(2,1)S(1)} %shard_map.112.refs_0_.refs_4_), channel_id=1, source_target_pairs={{0,1},{1,2},{2,3},{3,4},{4,5},{5,6},{6,7},{7,0},{8,9},{9,10},{10,1... | collective-permute-start | bytes 786440 | tf_op jit(solution)/shard_map/ppermute | solution.py:40
  97.4 17.2 %collective-permute-start.9 = (bf16[512,256]{1,0:T(8,128)(2,1)S(1)}, bf16[512,256]{1,0:T(8,128)(2,1)S(1)}, u32[]{:S(2)}, u32[]{:S(2)}) collective-permute-start(bf16[512,256]{1,0:T(8,128)(2,1)S(1)} %shard_map.112.refs_0_.refs_4_), channel_id=1, source_target_pairs={{0,2},{1,3},{2,4},{3,5},{4,6},{5,7},{6,0},{7,1},{8,10},{9,11},{10,... | collective-permute-start | bytes 786440 | tf_op jit(solution)/shard_map/ppermute | solution.py:40
  104.6 2.2 copy-start
  114.7 23.7 %copy-start.11 = (bf16[1,128,1024]{2,1,0:T(8,128)(2,1)S(1)}, bf16[1,128,1024]{2,1,0:T(8,128)(2,1)}, u32[]{:S(2)}) copy-start(bf16[1,128,1024]{2,1,0:T(8,128)(2,1)} %param.15) | copy-start | bytes 786436
  114.7 23.7 %copy-start.13 = (s32[1,1,128]{2,1,0:T(1,128)S(1)}, s32[1,1,128]{2,1,0:T(1,128)}, u32[]{:S(2)}) copy-start(s32[1,1,128]{2,1,0:T(1,128)} %param.14) | copy-start | bytes 1540
  119.4 10.3 %collective-permute-start.15 = (bf16[128,1408]{1,0:T(8,128)(2,1)S(1)}, bf16[128,1408]{1,0:T(8,128)(2,1)S(1)}, u32[]{:S(2)}, u32[]{:S(2)}) collective-permute-start(bf16[128,1408]{1,0:T(8,128)(2,1)S(1)} %get-tuple-element.23), channel_id=1, source_target_pairs={{0,8},{8,16},{16,24},{24,0},{1,9},{9,17},{17,25},{25,1},{2,10},{10... | collective-permute-start | bytes 1081352 | tf_op jit(solution)/shard_map/ppermute | solution.py:40
  120.4 17.8 %collective-permute-start.16 = (bf16[128,1408]{1,0:T(8,128)(2,1)S(1)}, bf16[128,1408]{1,0:T(8,128)(2,1)S(1)}, u32[]{:S(2)}, u32[]{:S(2)}) collective-permute-start(bf16[128,1408]{1,0:T(8,128)(2,1)S(1)} %get-tuple-element.24), channel_id=1, source_target_pairs={{0,16},{8,24},{16,0},{24,8},{1,17},{9,25},{17,1},{25,9},{2,18},{10... | collective-permute-start | bytes 1081352 | tf_op jit(solution)/shard_map/ppermute | solution.py:40
  122.7 15.7 %collective-permute-start.17 = (bf16[128,1408]{1,0:T(8,128)(2,1)S(1)}, bf16[128,1408]{1,0:T(8,128)(2,1)S(1)}, u32[]{:S(2)}, u32[]{:S(2)}) collective-permute-start(bf16[128,1408]{1,0:T(8,128)(2,1)S(1)} %get-tuple-element.25), channel_id=1, source_target_pairs={{0,24},{8,0},{16,8},{24,16},{1,25},{9,1},{17,9},{25,17},{2,26},{10... | collective-permute-start | bytes 1081352 | tf_op jit(solution)/shard_map/ppermute | solution.py:40
  140.6 11.2 %collective-permute-start.18 = (bf16[128,1408]{1,0:T(8,128)(2,1)S(1)}, bf16[128,1408]{1,0:T(8,128)(2,1)S(1)}, u32[]{:S(2)}, u32[]{:S(2)}) collective-permute-start(bf16[128,1408]{1,0:T(8,128)(2,1)S(1)} %get-tuple-element.27.refs_0_), channel_id=1, source_target_pairs={{0,8},{8,16},{16,24},{24,0},{1,9},{9,17},{17,25},{25,1},{2,10},{10... | collective-permute-start | bytes 1081352 | tf_op jit(solution)/shard_map/ppermute | solution.py:40
  142.6 18.4 %collective-permute-start.19 = (bf16[128,1408]{1,0:T(8,128)(2,1)S(1)}, bf16[128,1408]{1,0:T(8,128)(2,1)S(1)}, u32[]{:S(2)}, u32[]{:S(2)}) collective-permute-start(bf16[128,1408]{1,0:T(8,128)(2,1)S(1)} %get-tuple-element.27.refs_0_), channel_id=1, source_target_pairs={{0,16},{8,24},{16,0},{24,8},{1,17},{9,25},{17,1},{25,9},{2,18},{10... | collective-permute-start | bytes 1081352 | tf_op jit(solution)/shard_map/ppermute | solution.py:40
  145.3 15.7 %collective-permute-start.20 = (bf16[128,1408]{1,0:T(8,128)(2,1)S(1)}, bf16[128,1408]{1,0:T(8,128)(2,1)S(1)}, u32[]{:S(2)}, u32[]{:S(2)}) collective-permute-start(bf16[128,1408]{1,0:T(8,128)(2,1)S(1)} %get-tuple-element.27.refs_0_), channel_id=1, source_target_pairs={{0,24},{8,0},{16,8},{24,16},{1,25},{9,1},{17,9},{25,17},{2,26},{10... | collective-permute-start | bytes 1081352 | tf_op jit(solution)/shard_map/ppermute | solution.py:40
  194.0 46.7 %copy-start.1 = (bf16[1,256,1024]{2,1,0:T(8,128)(2,1)S(1)}, bf16[1,256,1024]{2,1,0:T(8,128)(2,1)}, u32[]{:S(2)}) copy-start(bf16[1,256,1024]{2,1,0:T(8,128)(2,1)} %param.9) | copy-start | bytes 1572868
  217.2 46.6 %copy-start.2 = (bf16[1,128,1024]{2,1,0:T(8,128)(2,1)S(1)}, bf16[1,128,1024]{2,1,0:T(8,128)(2,1)}, u32[]{:S(2)}) copy-start(bf16[1,128,1024]{2,1,0:T(8,128)(2,1)} %param.8) | copy-start | bytes 786436
  217.2 46.6 %copy-start.4 = (bf16[128,1024]{1,0:T(8,128)(2,1)S(1)}, bf16[128,1024]{1,0:T(8,128)(2,1)}, u32[]{:S(2)}) copy-start(bf16[128,1024]{1,0:T(8,128)(2,1)} %copy-done.3) | copy-start | bytes 786436
  217.2 46.6 %copy-start.6 = (bf16[128,1024]{1,0:T(8,128)(2,1)S(1)}, bf16[128,1024]{1,0:T(8,128)(2,1)}, u32[]{:S(2)}) copy-start(bf16[128,1024]{1,0:T(8,128)(2,1)} %copy-done.5) | copy-start | bytes 786436
  217.2 46.6 %copy-start.8 = (bf16[128,1024]{1,0:T(8,128)(2,1)S(1)}, bf16[128,1024]{1,0:T(8,128)(2,1)}, u32[]{:S(2)}) copy-start(bf16[128,1024]{1,0:T(8,128)(2,1)} %copy-done.7) | copy-start | bytes 786436
  218.7 8.5 %collective-permute-start.21 = (bf16[64,256]{1,0:T(8,128)(2,1)S(1)}, bf16[64,256]{1,0:T(8,128)(2,1)S(1)}, u32[]{:S(2)}, u32[]{:S(2)}) collective-permute-start(bf16[64,256]{1,0:T(8,128)(2,1)S(1)} %reduce_sum.25), channel_id=1, source_target_pairs={{0,224},{32,0},{64,32},{96,64},{128,96},{160,128},{192,160},{224,1... | collective-permute-start | bytes 98312 | tf_op jit(solution)/shard_map/ppermute | solution.py:36
  227.9 31.0 %all-to-all-start.4 = ((bf16[8,64,256]{2,1,0:T(8,128)(2,1)}), bf16[8,64,256]{2,1,0:T(8,128)(2,1)}, u32[]{:S(2)}, u32[]{:S(2)}) async-start(bf16[8,64,256]{2,1,0:T(8,128)(2,1)} %broadcast_in_dim.24), calls=%async_computation.4 | async-start | bytes 524288 | tf_op jit(solution)/shard_map/all_to_all | solution.py:28
  233.0 8.5 %collective-permute-start.25 = (bf16[256,256]{1,0:T(8,128)(2,1)S(1)}, bf16[256,256]{1,0:T(8,128)(2,1)S(1)}, u32[]{:S(2)}, u32[]{:S(2)}) collective-permute-start(bf16[256,256]{1,0:T(8,128)(2,1)S(1)} %get-tuple-element.32), channel_id=1, source_target_pairs={{0,0},{1,1},{8,2},{9,3},{16,4},{17,5},{24,6},{25,7},{2,8},{3,9},{1... | collective-permute-start | bytes 393224 | tf_op jit(solution)/shard_map/ppermute | solution.py:413
  233.7 20.3 %collective-permute-start.26 = (bf16[256,256]{1,0:T(8,128)(2,1)S(1)}, bf16[256,256]{1,0:T(8,128)(2,1)S(1)}, u32[]{:S(2)}, u32[]{:S(2)}) collective-permute-start(bf16[256,256]{1,0:T(8,128)(2,1)S(1)} %get-tuple-element.33), channel_id=1, source_target_pairs={{2,0},{3,1},{10,2},{11,3},{18,4},{19,5},{26,6},{27,7},{4,8},{5,9},... | collective-permute-start | bytes 393224 | tf_op jit(solution)/shard_map/ppermute | solution.py:413
  240.0 18.0 %collective-permute-start.27 = (bf16[256,256]{1,0:T(8,128)(2,1)S(1)}, bf16[256,256]{1,0:T(8,128)(2,1)S(1)}, u32[]{:S(2)}, u32[]{:S(2)}) collective-permute-start(bf16[256,256]{1,0:T(8,128)(2,1)S(1)} %get-tuple-element.34), channel_id=1, source_target_pairs={{4,0},{5,1},{12,2},{13,3},{20,4},{21,5},{28,6},{29,7},{6,8},{7,9},... | collective-permute-start | bytes 393224 | tf_op jit(solution)/shard_map/ppermute | solution.py:413
  240.6 17.3 %collective-permute-start.28 = (bf16[256,256]{1,0:T(8,128)(2,1)S(1)}, bf16[256,256]{1,0:T(8,128)(2,1)}, u32[]{:S(2)}, u32[]{:S(2)}) collective-permute-start(bf16[256,256]{1,0:T(8,128)(2,1)S(1)} %get-tuple-element.35), channel_id=1, source_target_pairs={{6,0},{7,1},{14,2},{15,3},{22,4},{23,5},{30,6},{31,7},{0,8},{1,9},... | collective-permute-start | bytes 393224 | tf_op jit(solution)/shard_map/ppermute | solution.py:413
  240.6 25.8 %collective-permute-start.22 = (bf16[256,1024]{1,0:T(8,128)(2,1)S(1)}, bf16[256,1024]{1,0:T(8,128)(2,1)S(1)}, u32[]{:S(2)}, u32[]{:S(2)}) collective-permute-start(bf16[256,1024]{1,0:T(8,128)(2,1)S(1)} %bitcast.33), channel_id=1, source_target_pairs={{0,8},{8,16},{16,24},{24,0},{1,9},{9,17},{17,25},{25,1},{2,10},{10... | collective-permute-start | bytes 1572872 | tf_op jit(solution)/shard_map/ppermute | solution.py:40
  241.5 26.9 %collective-permute-start.23 = (bf16[256,1024]{1,0:T(8,128)(2,1)S(1)}, bf16[256,1024]{1,0:T(8,128)(2,1)S(1)}, u32[]{:S(2)}, u32[]{:S(2)}) collective-permute-start(bf16[256,1024]{1,0:T(8,128)(2,1)S(1)} %bitcast.34), channel_id=1, source_target_pairs={{0,16},{8,24},{16,0},{24,8},{1,17},{9,25},{17,1},{25,9},{2,18},{10... | collective-permute-start | bytes 1572872 | tf_op jit(solution)/shard_map/ppermute | solution.py:40
  254.0 14.4 %collective-permute-start.24 = (bf16[256,1024]{1,0:T(8,128)(2,1)S(1)}, bf16[256,1024]{1,0:T(8,128)(2,1)}, u32[]{:S(2)}, u32[]{:S(2)}) collective-permute-start(bf16[256,1024]{1,0:T(8,128)(2,1)S(1)} %bitcast.35), channel_id=1, source_target_pairs={{0,24},{8,0},{16,8},{24,16},{1,25},{9,1},{17,9},{25,17},{2,26},{10... | collective-permute-start | bytes 1572872 | tf_op jit(solution)/shard_map/ppermute | solution.py:40
  259.0 10.7 %all-to-all-start.5 = ((bf16[4,128,256]{2,1,0:T(8,128)(2,1)}), bf16[4,128,256]{2,1,0:T(8,128)(2,1)S(1)}, u32[]{:S(2)}, u32[]{:S(2)}) async-start(bf16[4,128,256]{2,1,0:T(8,128)(2,1)} %bitcast.17), calls=%async_computation.5 | async-start | bytes 524288 | tf_op jit(solution)/shard_map/all_to_all | solution.py:28

commit v3 on v2

--- a/solution.py
+++ b/solution.py
@@ -73,19 +73,17 @@
     )(*args)
 
 
+def stage_code_kernel(place, own, encoder, rows, turned):
+    rows[...] = own[...]
+    turned[...] = encoder[...].T
+
+
 def code_kernel(place, *refs):
-    hidden, (encoder, code, rows, weight, ready) = refs[:F], refs[F:]
-    copies = [pltpu.make_async_copy(encoder, weight, ready.at[F])]
+    hidden, turned, code, rows = refs[:F], refs[F], refs[F + 1], refs[F + 2]
     for turn in range(F):
         row = pl.multiple_of(lax.rem(place[0] + F - turn, F) * 128, 128)
-        copies.append(
-            pltpu.make_async_copy(hidden[turn], rows.at[pl.ds(row, 128)], ready.at[turn])
-        )
-    for copy in copies:
-        copy.start()
-    for copy in copies:
-        copy.wait()
-    code[...] = mm(rows[...], weight[...], (1, 1)).astype(LOW)
+        rows[pl.ds(row, 128), :] = hidden[turn][...]
+    code[...] = mm(rows[...], turned[...], (1, 0)).astype(LOW)
 
 
 def decode_kernel(place, pieces, *refs):
@@ -289,8 +287,15 @@
         ).astype(LOW)
 
 
+def decoder_out_kernel(place, *refs):
+    blocks, decoder_grad = refs[:F], refs[F]
+    for turn in range(F):
+        lane = pl.multiple_of(lax.rem(place[0] + turn, F) * 256, 256)
+        decoder_grad[:, pl.ds(lane, 256)] = blocks[turn][...].astype(WIDE)
+
+
 def encoder_grad_kernel(place, columns, *refs):
-    hidden, encoder_grad = refs[:F], refs[F]
+    hidden, encoder, encoder_grad, staged = refs[:F], refs[F : 2 * F], refs[2 * F], refs[2 * F + 1]
     for turn in range(F):
         row = pl.multiple_of(lax.rem(place[0] + F - turn, F) * 128, 128)
         part = mm(columns[pl.ds(row, 128), :], hidden[turn][...], (0, 0))
@@ -298,14 +303,14 @@
             encoder_grad[...] = part
         else:
             encoder_grad[...] += part
-
-
-def hidden_grad_kernel(place, rows, *refs):
-    encoder, hidden_grad = refs[:F], refs[F]
-    total = mm(rows[place[0]], encoder[0][...], (1, 0))
+        staged[turn] = encoder[turn][...]
+
+
+def hidden_grad_kernel(place, *refs):
+    rows, staged, hidden_grad = refs[:F], refs[F], refs[F + 1]
+    total = mm(rows[0][...], staged[0], (1, 0))
     for turn in range(1, F):
-        part = rows[lax.rem(place[0] + F - turn, F)]
-        total = total + mm(part, encoder[turn][...], (1, 0))
+        total = total + mm(rows[turn][...], staged[turn], (1, 0))
     hidden_grad[...] = total.astype(LOW)
 
 
@@ -337,18 +342,18 @@
         decoder_parts.append(lax.ppermute(block, FT, column_route(turn)))
 
     small = 2 * 512 * 1024 * 256
+    own, turned_encoder = call(
+        stage_code_kernel,
+        [shape((128, 1024)), shape((1024, 256))],
+        [place, hidden[0], encoder],
+        0,
+    )
     (code_part,) = call(
         code_kernel,
         [shape((512, 256))],
-        [place, *hidden_parts, encoder],
+        [place, own, *hidden_parts[1:], turned_encoder],
         small,
-        [
-            pltpu.VMEM((512, 1024), LOW),
-            pltpu.VMEM((256, 1024), LOW),
-            pltpu.SemaphoreType.DMA((F + 1,)),
-        ],
-        far=F + 1,
-        grant=None,
+        [pltpu.VMEM((512, 1024), LOW)],
     )
     came = exchange(code_part.reshape(T, 64, 256), "tensor")
     code_piece = jnp.sum(came.astype(WIDE), axis=0).astype(LOW)
@@ -411,28 +416,24 @@
     for turn in range(F):
         back = [(target, source) for source, target in column_route(turn)]
         came.append(lax.ppermute(decoder_blocks[turn], FT, back))
-    came = jnp.stack(came)
-    decoder_grad = jnp.concatenate(
-        [
-            lax.dynamic_index_in_dim(came, (c + 4 - f) % 4, 0, keepdims=False)
-            for c in range(4)
-        ],
-        axis=1,
-    ).astype(WIDE)
+    (decoder_grad,) = call(
+        decoder_out_kernel, [shape((256, 1024), WIDE)], [place, *came], 0
+    )
 
     code_grad = spread(grad_moved, "tensor", T).reshape(512, 256)
-    grad_rows = exchange(code_grad.reshape(F, 128, 256), "fsdp")
-    (encoder_grad,) = call(
+    grad_rows = []
+    for turn in range(F):
+        start = lax.rem(f + turn, F) * 128
+        part = lax.dynamic_slice_in_dim(code_grad, start, 128, 0)
+        grad_rows.append(around(part, "fsdp", F, turn) if turn else part)
+    encoder_grad, staged = call(
         encoder_grad_kernel,
-        [shape((256, 1024), WIDE)],
-        [place, code_grad, *hidden_parts],
+        [shape((256, 1024), WIDE), shape((F, 256, 1024))],
+        [place, code_grad, *hidden_parts, *encoder_parts],
         small,
     )
     (hidden_grad,) = call(
-        hidden_grad_kernel,
-        [shape((128, 1024))],
-        [place, grad_rows, *encoder_parts],
-        small,
+        hidden_grad_kernel, [shape((128, 1024))], [place, *grad_rows, staged], small
     )
     return (mixed[None], hidden_grad[None], encoder_grad[None], decoder_grad[None])
 

time: 275 us -> 279 us (1.015)
  starting transfers between devices: 82.1 us -> 108 us
  blocking collectives: 63 us -> 40.9 us
  local copies, waits for them, and re-layouts: 4.94 us -> 9.33 us
    all_to_all x3 -> x2, blocking collectives: 63 us -> 40.9 us  [exchange(): return lax.all_to_all(blocks, axis, 0, 0)]
    ppermute x4, starting transfers between devices: 7.61 us -> 21.2 us  [section_step(): came.append(lax.ppermute(decoder_blocks[turn], FT, back))]
    all_to_all x3, waiting for transfers between devices: 1.33 us -> 14.3 us  [exchange(): return lax.all_to_all(blocks, axis, 0, 0)]
    ppermute x19 -> x22, starting transfers between devices: 42.4 us -> 52.3 us  [around(): lax.ppermute(value, axis, [(i, (i + turn) % count) for i in range(count)])]
    ppermute x4, waiting for transfers between devices: 9.83 us -> 0.01 us  [section_step(): came.append(lax.ppermute(decoder_blocks[turn], FT, back))]
    unnamed x30, local copies, waits for them, and re-layouts: 3.01 us -> 7.42 us
    ppermute x19 -> x22, waiting for transfers between devices: 54.8 us -> 50.8 us  [around(): lax.ppermute(value, axis, [(i, (i + turn) % count) for i in range(count)])]
    pallas_call x8 -> x10, Pallas kernels: 19.8 us -> 21.1 us  [call(): pl.pallas_call(kernel, out_shape=outs, in_specs=[SMEM] + [VMEM] * (len(ar...]
  transfers between devices with their start and end apart: 32 -> 35, of which waited for: 17 -> 14; matrix products, arithmetic and copies ran while one was open for 1% -> 1% of each run, Pallas kernels for 2% -> 3%
where the time goes in v3:
time: 279 us; the launch traced here: 278 us
  starting transfers between devices  108 us (39%)
  waiting for transfers between devices  92.3 us (33%)
  blocking collectives  40.9 us (15%)
  Pallas kernels  25.4 us (9%)
  local copies, waits for them, and re-layouts  9.33 us (3%)
    ppermute x22, starting transfers between devices, around(): lax.ppermute(value, axis, [(i, (i + turn) % count) for i in range(count)])  52.3 us
    ppermute x22, waiting for transfers between devices, around(): lax.ppermute(value, axis, [(i, (i + turn) % count) for i in range(count)])  50.8 us
    all_to_all x2, blocking collectives, exchange(): return lax.all_to_all(blocks, axis, 0, 0)  40.9 us
    ppermute x4, starting transfers between devices, section_step(): came.append(lax.ppermute(decoder_blocks[turn], FT, back))  21.2 us
    pallas_call x10, Pallas kernels, call(): pl.pallas_call(kernel, out_shape=outs, in_specs=[SMEM] + [VMEM] * (len(ar...  21.1 us
    ppermute x4, waiting for transfers between devices, section_step(): decoder_parts.append(lax.ppermute(block, FT, column_route(turn)))  20.4 us
    all_to_all x3, starting transfers between devices, exchange(): return lax.all_to_all(blocks, axis, 0, 0)  14.8 us
    all_to_all x3, waiting for transfers between devices, exchange(): return lax.all_to_all(blocks, axis, 0, 0)  14.3 us
  transfers between devices with their start and end apart: 35, of which 14 were waited for; matrix products, arithmetic and copies ran while one was open for 1% of the time, Pallas kernels for 3%

profile of v3, /device:TPU:1, one launch (start us, length us, event | category | flops | bytes accessed | tf_op | source)
XLA Modules:
  0.0 278.0 jit_solution(935764423564117727)
XLA Ops:
  0.6 2.1 collective-permute-start
  2.7 2.5 collective-permute-start.1
  9.2 7.6 %collective-permute-done.1.refs_2_ = bf16[128,1024]{1,0:T(8,128)(2,1)S(1)} collective-permute-done((bf16[128,1024]{1,0:T(8,128)(2,1)}, bf16[128,1024]{1,0:T(8,128)(2,1)S(1)}, u32[]{:S(2)}, u32[]{:S(2)}) %collective-permute-start.1) | collective-permute-done | bytes 262176 | tf_op jit(solution)/shard_map/ppermute | solution.py:40
  17.8 11.5 %all_to_all.25 = bf16[8,64,256]{2,1,0:T(8,128)(2,1)S(1)} all-to-all(bf16[8,64,256]{2,1,0:T(8,128)(2,1)S(1)} %bitcast.40), channel_id=1, replica_groups=mesh['section'=8,'fsdp'=4,'tensor'=8] {'tensor'}, dimensions={0} | all-to-all | bytes 524288 | tf_op jit(solution)/shard_map/all_to_all | solution.py:28
  29.3 5.9 %collective-permute-start.3 = (bf16[64,256]{1,0:T(8,128)(2,1)S(1)}, bf16[64,256]{1,0:T(8,128)(2,1)S(1)}, u32[]{:S(2)}, u32[]{:S(2)}) collective-permute-start(bf16[64,256]{1,0:T(8,128)(2,1)S(1)} %reduce_sum.24), channel_id=1, source_target_pairs={{0,32},{32,64},{64,96},{96,128},{128,160},{160,192},{192,224},{224... | collective-permute-start | bytes 98312 | tf_op jit(solution)/shard_map/ppermute | solution.py:36
  37.3 4.9 %all-to-all-start.1 = ((bf16[32,64,256]{2,1,0:T(8,128)(2,1)}), bf16[32,64,256]{2,1,0:T(8,128)(2,1)S(1)}, u32[]{:S(2)}, u32[]{:S(2)}) async-start(bf16[32,64,256]{2,1,0:T(8,128)(2,1)} %broadcast_in_dim.24), calls=%async_computation.1 | async-start | bytes 2097152 | tf_op jit(solution)/shard_map/all_to_all | solution.py:28
  43.1 3.7 %collective-permute-start.5 = (bf16[256,256]{1,0:T(8,128)(2,1)S(1)}, bf16[256,256]{1,0:T(8,128)(2,1)S(1)}, u32[]{:S(2)}, u32[]{:S(2)}) collective-permute-start(bf16[256,256]{1,0:T(8,128)(2,1)S(1)} %get-tuple-element.45), channel_id=1, source_target_pairs={{0,2},{1,3},{2,10},{3,11},{4,18},{5,19},{6,26},{7,27},{8,4},{9,5},... | collective-permute-start | bytes 393224 | tf_op jit(solution)/shard_map/ppermute | solution.py:342
  46.8 4.2 %collective-permute-start.6 = (bf16[256,256]{1,0:T(8,128)(2,1)S(1)}, bf16[256,256]{1,0:T(8,128)(2,1)S(1)}, u32[]{:S(2)}, u32[]{:S(2)}) collective-permute-start(bf16[256,256]{1,0:T(8,128)(2,1)S(1)} %get-tuple-element.47), channel_id=1, source_target_pairs={{0,4},{1,5},{2,12},{3,13},{4,20},{5,21},{6,28},{7,29},{8,6},{9,7},... | collective-permute-start | bytes 393224 | tf_op jit(solution)/shard_map/ppermute | solution.py:342
  51.0 1.8 collective-permute-start.7
  52.8 20.4 %collective-permute-done.5.refs_1_.refs_2_ = bf16[256,256]{1,0:T(8,128)(2,1)S(1)} collective-permute-done((bf16[256,256]{1,0:T(8,128)(2,1)S(1)}, bf16[256,256]{1,0:T(8,128)(2,1)S(1)}, u32[]{:S(2)}, u32[]{:S(2)}) %collective-permute-start.5) | collective-permute-done | bytes 131104 | tf_op jit(solution)/shard_map/ppermute | solution.py:342
  75.8 5.1 %collective-permute-start.10 = (bf16[512,256]{1,0:T(8,128)(2,1)S(1)}, bf16[512,256]{1,0:T(8,128)(2,1)S(1)}, u32[]{:S(2)}, u32[]{:S(2)}) collective-permute-start(bf16[512,256]{1,0:T(8,128)(2,1)S(1)} %shard_map.113.refs_0_.refs_4_), channel_id=1, source_target_pairs={{0,3},{1,4},{2,5},{3,6},{4,7},{5,0},{6,1},{7,2},{8,11},{9,12},{10,... | collective-permute-start | bytes 786440 | tf_op jit(solution)/shard_map/ppermute | solution.py:40
  80.8 3.4 %collective-permute-start.11 = (bf16[512,256]{1,0:T(8,128)(2,1)S(1)}, bf16[512,256]{1,0:T(8,128)(2,1)S(1)}, u32[]{:S(2)}, u32[]{:S(2)}) collective-permute-start(bf16[512,256]{1,0:T(8,128)(2,1)S(1)} %shard_map.113.refs_0_.refs_4_), channel_id=1, source_target_pairs={{0,4},{1,5},{2,6},{3,7},{4,0},{5,1},{6,2},{7,3},{8,12},{9,13},{10,... | collective-permute-start | bytes 786440 | tf_op jit(solution)/shard_map/ppermute | solution.py:40
  84.2 3.8 %collective-permute-start.12 = (bf16[512,256]{1,0:T(8,128)(2,1)S(1)}, bf16[512,256]{1,0:T(8,128)(2,1)S(1)}, u32[]{:S(2)}, u32[]{:S(2)}) collective-permute-start(bf16[512,256]{1,0:T(8,128)(2,1)S(1)} %shard_map.113.refs_0_.refs_4_), channel_id=1, source_target_pairs={{0,5},{1,6},{2,7},{3,0},{4,1},{5,2},{6,3},{7,4},{8,13},{9,14},{10,... | collective-permute-start | bytes 786440 | tf_op jit(solution)/shard_map/ppermute | solution.py:40
  88.3 2.3 collective-permute-done.10.refs_3_.refs_7_
  90.6 5.1 %collective-permute-done.11.refs_4_.refs_8_ = bf16[512,256]{1,0:T(8,128)(2,1)S(1)} collective-permute-done((bf16[512,256]{1,0:T(8,128)(2,1)S(1)}, bf16[512,256]{1,0:T(8,128)(2,1)S(1)}, u32[]{:S(2)}, u32[]{:S(2)}) %collective-permute-start.11) | collective-permute-done | bytes 262176 | tf_op jit(solution)/shard_map/ppermute | solution.py:40
  95.7 7.2 %collective-permute-start.9 = (bf16[512,256]{1,0:T(8,128)(2,1)S(1)}, bf16[512,256]{1,0:T(8,128)(2,1)S(1)}, u32[]{:S(2)}, u32[]{:S(2)}) collective-permute-start(bf16[512,256]{1,0:T(8,128)(2,1)S(1)} %shard_map.113.refs_0_.refs_4_), channel_id=1, source_target_pairs={{0,2},{1,3},{2,4},{3,5},{4,6},{5,7},{6,0},{7,1},{8,10},{9,11},{10,... | collective-permute-start | bytes 786440 | tf_op jit(solution)/shard_map/ppermute | solution.py:40
  102.9 2.2 copy-done
  105.1 1.9 stage_weights.1
  107.0 1.6 collective-permute-done.13.refs_6_.refs_10_
  108.6 4.3 %collective-permute-done.9.refs_2_.refs_6_ = bf16[512,256]{1,0:T(8,128)(2,1)S(1)} collective-permute-done((bf16[512,256]{1,0:T(8,128)(2,1)S(1)}, bf16[512,256]{1,0:T(8,128)(2,1)S(1)}, u32[]{:S(2)}, u32[]{:S(2)}) %collective-permute-start.9) | collective-permute-done | bytes 262176 | tf_op jit(solution)/shard_map/ppermute | solution.py:40
  113.0 4.8 %shard_map.114 = (bf16[128,1408]{1,0:T(8,128)(2,1)S(1)}, bf16[128,1408]{1,0:T(8,128)(2,1)S(1)}, bf16[128,1408]{1,0:T(8,128)(2,1)S(1)}, bf16[128,1408]{1,0:T(8,128)(2,1)S(1)}) custom-call(s32[2]{0:T(128)S(1)} %pad_add_fusion.place, bf16[512,256]{1,0:T(8,128)(2,1)S(1)} %shard_map.113.refs_0_.refs_4_, ...), custom_call_target="tpu_custom_call" | custom-call | flops 2684354560 | bytes 7340040 | tf_op jit(solution)/shard_map/pallas_call | solution.py:63
  118.8 2.2 collective-permute-start.16
  121.0 1.5 collective-permute-start.17
  122.5 5.6 %collective-permute-done.15.refs_1_ = bf16[128,1408]{1,0:T(8,128)(2,1)S(1)} collective-permute-done((bf16[128,1408]{1,0:T(8,128)(2,1)S(1)}, bf16[128,1408]{1,0:T(8,128)(2,1)S(1)}, u32[]{:S(2)}, u32[]{:S(2)}) %collective-permute-start.15) | collective-permute-done | bytes 360480 | tf_op jit(solution)/shard_map/ppermute | solution.py:40
  128.1 8.5 %collective-permute-done.16.refs_2_ = bf16[128,1408]{1,0:T(8,128)(2,1)S(1)} collective-permute-done((bf16[128,1408]{1,0:T(8,128)(2,1)S(1)}, bf16[128,1408]{1,0:T(8,128)(2,1)S(1)}, u32[]{:S(2)}, u32[]{:S(2)}) %collective-permute-start.16) | collective-permute-done | bytes 360480 | tf_op jit(solution)/shard_map/ppermute | solution.py:40
  136.6 2.3 attention_stage.1
  138.9 2.0 collective-permute-start.18
  141.0 2.6 collective-permute-start.19
  143.7 6.5 %collective-permute-done.18.refs_1_ = bf16[128,1408]{1,0:T(8,128)(2,1)S(1)} collective-permute-done((bf16[128,1408]{1,0:T(8,128)(2,1)S(1)}, bf16[128,1408]{1,0:T(8,128)(2,1)S(1)}, u32[]{:S(2)}, u32[]{:S(2)}) %collective-permute-start.18) | collective-permute-done | bytes 360480 | tf_op jit(solution)/shard_map/ppermute | solution.py:40
  150.1 9.2 %collective-permute-done.19.refs_2_ = bf16[128,1408]{1,0:T(8,128)(2,1)S(1)} collective-permute-done((bf16[128,1408]{1,0:T(8,128)(2,1)S(1)}, bf16[128,1408]{1,0:T(8,128)(2,1)S(1)}, u32[]{:S(2)}, u32[]{:S(2)}) %collective-permute-start.19) | collective-permute-done | bytes 360480 | tf_op jit(solution)/shard_map/ppermute | solution.py:40
  159.3 3.7 %shard_map.115 = bf16[8,512,256]{2,1,0:T(8,128)(2,1)S(1)} custom-call(s32[2]{0:T(128)S(1)} %pad_add_fusion.place, bf16[128,1408]{1,0:T(8,128)(2,1)S(1)} %get-tuple-element.33.refs_0_, bf16[128,1408]{1,0:T(8,128)(2,1)S(1)} %collective-permute-done.18.refs_1_, bf16[128,1408]{1,0:T(8,128)(2,1)S(1)} %collective-permute-done.19.refs_2_, ...), custom_call_target="tpu_custom_call" | custom-call | flops 2684354560 | bytes 8781832 | tf_op jit(solution)/shard_map/pallas_call | solution.py:63
  163.1 29.4 %all_to_all.26.refs_0_ = bf16[8,512,256]{2,1,0:T(8,128)(2,1)S(1)} all-to-all(bf16[8,512,256]{2,1,0:T(8,128)(2,1)S(1)} %shard_map.115), channel_id=1, replica_groups=mesh['section'=8,'fsdp'=4,'tensor'=8] {'tensor'}, dimensions={0} | all-to-all | bytes 4194304 | tf_op jit(solution)/shard_map/all_to_all | solution.py:28
  192.4 2.1 shard_map.116
  195.2 6.5 %all-to-all-start.3 = ((bf16[32,64,256]{2,1,0:T(8,128)(2,1)}), bf16[32,64,256]{2,1,0:T(8,128)(2,1)}, u32[]{:S(2)}, u32[]{:S(2)}) async-start(bf16[32,64,256]{2,1,0:T(8,128)(2,1)} %bitcast.16), calls=%async_computation.3 | async-start | bytes 2097152 | tf_op jit(solution)/shard_map/all_to_all | solution.py:28
  203.2 14.3 %all-to-all-done.3 = bf16[32,64,256]{2,1,0:T(8,128)(2,1)} async-done(((bf16[32,64,256]{2,1,0:T(8,128)(2,1)}), bf16[32,64,256]{2,1,0:T(8,128)(2,1)}, u32[]{:S(2)}, u32[]{:S(2)}) %all-to-all-start.3) | async-done | bytes 1048608 | tf_op jit(solution)/shard_map/all_to_all | solution.py:28
  218.9 3.1 %collective-permute-start.21 = (bf16[64,256]{1,0:T(8,128)(2,1)S(1)}, bf16[64,256]{1,0:T(8,128)(2,1)S(1)}, u32[]{:S(2)}, u32[]{:S(2)}) collective-permute-start(bf16[64,256]{1,0:T(8,128)(2,1)S(1)} %reduce_sum.25), channel_id=1, source_target_pairs={{0,224},{32,0},{64,32},{96,64},{128,96},{160,128},{192,160},{224,1... | collective-permute-start | bytes 98312 | tf_op jit(solution)/shard_map/ppermute | solution.py:36
  222.0 5.7 %collective-permute-done.21 = bf16[64,256]{1,0:T(8,128)(2,1)S(1)} collective-permute-done((bf16[64,256]{1,0:T(8,128)(2,1)S(1)}, bf16[64,256]{1,0:T(8,128)(2,1)S(1)}, u32[]{:S(2)}, u32[]{:S(2)}) %collective-permute-start.21) | collective-permute-done | bytes 32800 | tf_op jit(solution)/shard_map/ppermute | solution.py:36
  228.4 3.4 %all-to-all-start.4 = ((bf16[8,64,256]{2,1,0:T(8,128)(2,1)}), bf16[8,64,256]{2,1,0:T(8,128)(2,1)S(1)}, u32[]{:S(2)}, u32[]{:S(2)}) async-start(bf16[8,64,256]{2,1,0:T(8,128)(2,1)} %broadcast_in_dim.26), calls=%async_computation.4 | async-start | bytes 524288 | tf_op jit(solution)/shard_map/all_to_all | solution.py:28
  233.7 1.7 shard_map.119
  236.0 6.4 %collective-permute-start.29 = (bf16[256,256]{1,0:T(8,128)(2,1)}, bf16[256,256]{1,0:T(8,128)(2,1)S(1)}, u32[]{:S(2)}, u32[]{:S(2)}) collective-permute-start(bf16[256,256]{1,0:T(8,128)(2,1)} %get-tuple-element.41), channel_id=1, source_target_pairs={{2,0},{3,1},{10,2},{11,3},{18,4},{19,5},{26,6},{27,7},{4,8},{5,9},... | collective-permute-start | bytes 393224 | tf_op jit(solution)/shard_map/ppermute | solution.py:418
  242.4 1.7 collective-permute-start.30
  244.1 12.4 %collective-permute-start.31 = (bf16[256,256]{1,0:T(8,128)(2,1)S(1)}, bf16[256,256]{1,0:T(8,128)(2,1)S(1)}, u32[]{:S(2)}, u32[]{:S(2)}) collective-permute-start(bf16[256,256]{1,0:T(8,128)(2,1)S(1)} %get-tuple-element.43), channel_id=1, source_target_pairs={{6,0},{7,1},{14,2},{15,3},{22,4},{23,5},{30,6},{31,7},{0,8},{1,9},... | collective-permute-start | bytes 393224 | tf_op jit(solution)/shard_map/ppermute | solution.py:418
  256.6 1.5 collective-permute-start.22
  258.1 6.7 %collective-permute-start.23 = (bf16[128,256]{1,0:T(8,128)(2,1)S(1)}, bf16[128,256]{1,0:T(8,128)(2,1)S(1)}, u32[]{:S(2)}, u32[]{:S(2)}) collective-permute-start(bf16[128,256]{1,0:T(8,128)(2,1)S(1)} %get-tuple-element.49), channel_id=1, source_target_pairs={{0,16},{8,24},{16,0},{24,8},{1,17},{9,25},{17,1},{25,9},{2,18},{10... | collective-permute-start | bytes 196616 | tf_op jit(solution)/shard_map/ppermute | solution.py:40
  264.8 7.0 %collective-permute-start.24 = (bf16[128,256]{1,0:T(8,128)(2,1)S(1)}, bf16[128,256]{1,0:T(8,128)(2,1)S(1)}, u32[]{:S(2)}, u32[]{:S(2)}) collective-permute-start(bf16[128,256]{1,0:T(8,128)(2,1)S(1)} %get-tuple-element.48), channel_id=1, source_target_pairs={{0,24},{8,0},{16,8},{24,16},{1,25},{9,1},{17,9},{25,17},{2,26},{10... | collective-permute-start | bytes 196616 | tf_op jit(solution)/shard_map/ppermute | solution.py:40
  271.8 1.6 shard_map.120
  273.4 2.9 %shard_map.117 = (f32[256,1024]{1,0:T(8,128)}, bf16[4,256,1024]{2,1,0:T(8,128)(2,1)S(1)}) custom-call(s32[2]{0:T(128)S(1)} %pad_add_fusion.place, bf16[512,256]{1,0:T(8,128)(2,1)S(1)} %bitcast.29, bf16[128,1024]{1,0:T(8,128)(2,1)S(1)} %bitcast.39, bf16[128,1024]{1,0:T(8,128)(2,1)S(1)} %collective-permute-done.refs_1_, ...), custom_call_target="tpu_custom_call" | custom-call | flops 268435456 | bytes 3407880 | tf_op jit(solution)/shard_map/pallas_call | solution.py:63
  276.3 1.7 shard_map.118
  (73 shorter events, 18.7 us)
Async XLA Ops:
  0.6 8.5 %collective-permute-start = (bf16[128,1024]{1,0:T(8,128)(2,1)}, bf16[128,1024]{1,0:T(8,128)(2,1)S(1)}, u32[]{:S(2)}, u32[]{:S(2)}) collective-permute-start(bf16[128,1024]{1,0:T(8,128)(2,1)} %bitcast.35), channel_id=1, source_target_pairs={{0,8},{8,16},{16,24},{24,0},{1,9},{9,17},{17,25},{25,1},{2,10},{10... | collective-permute-start | bytes 786440 | tf_op jit(solution)/shard_map/ppermute | solution.py:40
  2.7 14.0 %collective-permute-start.1 = (bf16[128,1024]{1,0:T(8,128)(2,1)}, bf16[128,1024]{1,0:T(8,128)(2,1)S(1)}, u32[]{:S(2)}, u32[]{:S(2)}) collective-permute-start(bf16[128,1024]{1,0:T(8,128)(2,1)} %bitcast.36), channel_id=1, source_target_pairs={{0,16},{8,24},{16,0},{24,8},{1,17},{9,25},{17,1},{25,9},{2,18},{10... | collective-permute-start | bytes 786440 | tf_op jit(solution)/shard_map/ppermute | solution.py:40
  5.2 11.6 %collective-permute-start.2 = (bf16[128,1024]{1,0:T(8,128)(2,1)}, bf16[128,1024]{1,0:T(8,128)(2,1)S(1)}, u32[]{:S(2)}, u32[]{:S(2)}) collective-permute-start(bf16[128,1024]{1,0:T(8,128)(2,1)} %bitcast.37), channel_id=1, source_target_pairs={{0,24},{8,0},{16,8},{24,16},{1,25},{9,1},{17,9},{25,17},{2,26},{10... | collective-permute-start | bytes 786440 | tf_op jit(solution)/shard_map/ppermute | solution.py:40
  6.4 1.0 copy-start.1
  7.5 0.9 copy-start.3
  8.4 33.9 %copy-start.14 = (bf16[1,256,1024]{2,1,0:T(8,128)(2,1)S(1)}, bf16[1,256,1024]{2,1,0:T(8,128)(2,1)}, u32[]{:S(2)}) copy-start(bf16[1,256,1024]{2,1,0:T(8,128)(2,1)} %param.10) | copy-start | bytes 1572868
  16.7 86.1 %copy-start.5 = (bf16[1,2048,128]{2,1,0:T(8,128)(2,1)S(1)}, bf16[1,2048,128]{2,1,0:T(8,128)(2,1)}, u32[]{:S(2)}) copy-start(bf16[1,2048,128]{2,1,0:T(8,128)(2,1)} %param.12) | copy-start | bytes 1572868
  16.7 86.1 %copy-start.6 = (bf16[1,2048,128]{2,1,0:T(8,128)(2,1)S(1)}, bf16[1,2048,128]{2,1,0:T(8,128)(2,1)}, u32[]{:S(2)}) copy-start(bf16[1,2048,128]{2,1,0:T(8,128)(2,1)} %param.13) | copy-start | bytes 1572868
  29.3 6.9 %collective-permute-start.3 = (bf16[64,256]{1,0:T(8,128)(2,1)S(1)}, bf16[64,256]{1,0:T(8,128)(2,1)S(1)}, u32[]{:S(2)}, u32[]{:S(2)}) collective-permute-start(bf16[64,256]{1,0:T(8,128)(2,1)S(1)} %reduce_sum.24), channel_id=1, source_target_pairs={{0,32},{32,64},{64,96},{96,128},{128,160},{160,192},{192,224},{224... | collective-permute-start | bytes 98312 | tf_op jit(solution)/shard_map/ppermute | solution.py:36
  37.3 36.5 %all-to-all-start.1 = ((bf16[32,64,256]{2,1,0:T(8,128)(2,1)}), bf16[32,64,256]{2,1,0:T(8,128)(2,1)S(1)}, u32[]{:S(2)}, u32[]{:S(2)}) async-start(bf16[32,64,256]{2,1,0:T(8,128)(2,1)} %broadcast_in_dim.24), calls=%async_computation.1 | async-start | bytes 2097152 | tf_op jit(solution)/shard_map/all_to_all | solution.py:28
  42.4 10.4 %collective-permute-start.4 = (bf16[256,256]{1,0:T(8,128)(2,1)S(1)}, bf16[256,256]{1,0:T(8,128)(2,1)S(1)}, u32[]{:S(2)}, u32[]{:S(2)}) collective-permute-start(bf16[256,256]{1,0:T(8,128)(2,1)S(1)} %get-tuple-element.46), channel_id=1, source_target_pairs={{0,0},{1,1},{2,8},{3,9},{4,16},{5,17},{6,24},{7,25},{8,2},{9,3},{1... | collective-permute-start | bytes 393224 | tf_op jit(solution)/shard_map/ppermute | solution.py:342
  43.1 30.1 %collective-permute-start.5 = (bf16[256,256]{1,0:T(8,128)(2,1)S(1)}, bf16[256,256]{1,0:T(8,128)(2,1)S(1)}, u32[]{:S(2)}, u32[]{:S(2)}) collective-permute-start(bf16[256,256]{1,0:T(8,128)(2,1)S(1)} %get-tuple-element.45), channel_id=1, source_target_pairs={{0,2},{1,3},{2,10},{3,11},{4,18},{5,19},{6,26},{7,27},{8,4},{9,5},... | collective-permute-start | bytes 393224 | tf_op jit(solution)/shard_map/ppermute | solution.py:342
  46.8 26.4 %collective-permute-start.6 = (bf16[256,256]{1,0:T(8,128)(2,1)S(1)}, bf16[256,256]{1,0:T(8,128)(2,1)S(1)}, u32[]{:S(2)}, u32[]{:S(2)}) collective-permute-start(bf16[256,256]{1,0:T(8,128)(2,1)S(1)} %get-tuple-element.47), channel_id=1, source_target_pairs={{0,4},{1,5},{2,12},{3,13},{4,20},{5,21},{6,28},{7,29},{8,6},{9,7},... | collective-permute-start | bytes 393224 | tf_op jit(solution)/shard_map/ppermute | solution.py:342
  51.0 22.2 %collective-permute-start.7 = (bf16[256,256]{1,0:T(8,128)(2,1)S(1)}, bf16[256,256]{1,0:T(8,128)(2,1)S(1)}, u32[]{:S(2)}, u32[]{:S(2)}) collective-permute-start(bf16[256,256]{1,0:T(8,128)(2,1)S(1)} %get-tuple-element.44), channel_id=1, source_target_pairs={{0,6},{1,7},{2,14},{3,15},{4,22},{5,23},{6,30},{7,31},{8,0},{9,1},... | collective-permute-start | bytes 393224 | tf_op jit(solution)/shard_map/ppermute | solution.py:342
  73.9 0.9 copy-start.8
  75.8 14.9 %collective-permute-start.10 = (bf16[512,256]{1,0:T(8,128)(2,1)S(1)}, bf16[512,256]{1,0:T(8,128)(2,1)S(1)}, u32[]{:S(2)}, u32[]{:S(2)}) collective-permute-start(bf16[512,256]{1,0:T(8,128)(2,1)S(1)} %shard_map.113.refs_0_.refs_4_), channel_id=1, source_target_pairs={{0,3},{1,4},{2,5},{3,6},{4,7},{5,0},{6,1},{7,2},{8,11},{9,12},{10,... | collective-permute-start | bytes 786440 | tf_op jit(solution)/shard_map/ppermute | solution.py:40
  80.8 14.9 %collective-permute-start.11 = (bf16[512,256]{1,0:T(8,128)(2,1)S(1)}, bf16[512,256]{1,0:T(8,128)(2,1)S(1)}, u32[]{:S(2)}, u32[]{:S(2)}) collective-permute-start(bf16[512,256]{1,0:T(8,128)(2,1)S(1)} %shard_map.113.refs_0_.refs_4_), channel_id=1, source_target_pairs={{0,4},{1,5},{2,6},{3,7},{4,0},{5,1},{6,2},{7,3},{8,12},{9,13},{10,... | collective-permute-start | bytes 786440 | tf_op jit(solution)/shard_map/ppermute | solution.py:40
  84.2 22.8 %collective-permute-start.12 = (bf16[512,256]{1,0:T(8,128)(2,1)S(1)}, bf16[512,256]{1,0:T(8,128)(2,1)S(1)}, u32[]{:S(2)}, u32[]{:S(2)}) collective-permute-start(bf16[512,256]{1,0:T(8,128)(2,1)S(1)} %shard_map.113.refs_0_.refs_4_), channel_id=1, source_target_pairs={{0,5},{1,6},{2,7},{3,0},{4,1},{5,2},{6,3},{7,4},{8,13},{9,14},{10,... | collective-permute-start | bytes 786440 | tf_op jit(solution)/shard_map/ppermute | solution.py:40
  88.0 20.6 %collective-permute-start.13 = (bf16[512,256]{1,0:T(8,128)(2,1)S(1)}, bf16[512,256]{1,0:T(8,128)(2,1)S(1)}, u32[]{:S(2)}, u32[]{:S(2)}) collective-permute-start(bf16[512,256]{1,0:T(8,128)(2,1)S(1)} %shard_map.113.refs_0_.refs_4_), channel_id=1, source_target_pairs={{0,6},{1,7},{2,0},{3,1},{4,2},{5,3},{6,4},{7,5},{8,14},{9,15},{10,... | collective-permute-start | bytes 786440 | tf_op jit(solution)/shard_map/ppermute | solution.py:40
  88.0 20.6 %collective-permute-start.14 = (bf16[512,256]{1,0:T(8,128)(2,1)S(1)}, bf16[512,256]{1,0:T(8,128)(2,1)S(1)}, u32[]{:S(2)}, u32[]{:S(2)}) collective-permute-start(bf16[512,256]{1,0:T(8,128)(2,1)S(1)} %shard_map.113.refs_0_.refs_4_), channel_id=1, source_target_pairs={{0,7},{1,0},{2,1},{3,2},{4,3},{5,4},{6,5},{7,6},{8,15},{9,8},{10,9... | collective-permute-start | bytes 786440 | tf_op jit(solution)/shard_map/ppermute | solution.py:40
  90.6 18.0 %collective-permute-start.8 = (bf16[512,256]{1,0:T(8,128)(2,1)S(1)}, bf16[512,256]{1,0:T(8,128)(2,1)S(1)}, u32[]{:S(2)}, u32[]{:S(2)}) collective-permute-start(bf16[512,256]{1,0:T(8,128)(2,1)S(1)} %shard_map.113.refs_0_.refs_4_), channel_id=1, source_target_pairs={{0,1},{1,2},{2,3},{3,4},{4,5},{5,6},{6,7},{7,0},{8,9},{9,10},{10,1... | collective-permute-start | bytes 786440 | tf_op jit(solution)/shard_map/ppermute | solution.py:40
  95.7 17.2 %collective-permute-start.9 = (bf16[512,256]{1,0:T(8,128)(2,1)S(1)}, bf16[512,256]{1,0:T(8,128)(2,1)S(1)}, u32[]{:S(2)}, u32[]{:S(2)}) collective-permute-start(bf16[512,256]{1,0:T(8,128)(2,1)S(1)} %shard_map.113.refs_0_.refs_4_), channel_id=1, source_target_pairs={{0,2},{1,3},{2,4},{3,5},{4,6},{5,7},{6,0},{7,1},{8,10},{9,11},{10,... | collective-permute-start | bytes 786440 | tf_op jit(solution)/shard_map/ppermute | solution.py:40
  102.9 2.2 copy-start
  113.0 23.7 %copy-start.10 = (bf16[1,128,1024]{2,1,0:T(8,128)(2,1)S(1)}, bf16[1,128,1024]{2,1,0:T(8,128)(2,1)}, u32[]{:S(2)}) copy-start(bf16[1,128,1024]{2,1,0:T(8,128)(2,1)} %param.15) | copy-start | bytes 786436
  113.0 23.7 %copy-start.13 = (s32[1,1,128]{2,1,0:T(1,128)S(1)}, s32[1,1,128]{2,1,0:T(1,128)}, u32[]{:S(2)}) copy-start(s32[1,1,128]{2,1,0:T(1,128)} %param.14) | copy-start | bytes 1540
  117.7 10.3 %collective-permute-start.15 = (bf16[128,1408]{1,0:T(8,128)(2,1)S(1)}, bf16[128,1408]{1,0:T(8,128)(2,1)S(1)}, u32[]{:S(2)}, u32[]{:S(2)}) collective-permute-start(bf16[128,1408]{1,0:T(8,128)(2,1)S(1)} %get-tuple-element.29), channel_id=1, source_target_pairs={{0,8},{8,16},{16,24},{24,0},{1,9},{9,17},{17,25},{25,1},{2,10},{10... | collective-permute-start | bytes 1081352 | tf_op jit(solution)/shard_map/ppermute | solution.py:40
  118.8 17.8 %collective-permute-start.16 = (bf16[128,1408]{1,0:T(8,128)(2,1)S(1)}, bf16[128,1408]{1,0:T(8,128)(2,1)S(1)}, u32[]{:S(2)}, u32[]{:S(2)}) collective-permute-start(bf16[128,1408]{1,0:T(8,128)(2,1)S(1)} %get-tuple-element.30), channel_id=1, source_target_pairs={{0,16},{8,24},{16,0},{24,8},{1,17},{9,25},{17,1},{25,9},{2,18},{10... | collective-permute-start | bytes 1081352 | tf_op jit(solution)/shard_map/ppermute | solution.py:40
  121.0 15.7 %collective-permute-start.17 = (bf16[128,1408]{1,0:T(8,128)(2,1)S(1)}, bf16[128,1408]{1,0:T(8,128)(2,1)S(1)}, u32[]{:S(2)}, u32[]{:S(2)}) collective-permute-start(bf16[128,1408]{1,0:T(8,128)(2,1)S(1)} %get-tuple-element.31), channel_id=1, source_target_pairs={{0,24},{8,0},{16,8},{24,16},{1,25},{9,1},{17,9},{25,17},{2,26},{10... | collective-permute-start | bytes 1081352 | tf_op jit(solution)/shard_map/ppermute | solution.py:40
  138.9 11.2 %collective-permute-start.18 = (bf16[128,1408]{1,0:T(8,128)(2,1)S(1)}, bf16[128,1408]{1,0:T(8,128)(2,1)S(1)}, u32[]{:S(2)}, u32[]{:S(2)}) collective-permute-start(bf16[128,1408]{1,0:T(8,128)(2,1)S(1)} %get-tuple-element.33.refs_0_), channel_id=1, source_target_pairs={{0,8},{8,16},{16,24},{24,0},{1,9},{9,17},{17,25},{25,1},{2,10},{10... | collective-permute-start | bytes 1081352 | tf_op jit(solution)/shard_map/ppermute | solution.py:40
  141.0 18.4 %collective-permute-start.19 = (bf16[128,1408]{1,0:T(8,128)(2,1)S(1)}, bf16[128,1408]{1,0:T(8,128)(2,1)S(1)}, u32[]{:S(2)}, u32[]{:S(2)}) collective-permute-start(bf16[128,1408]{1,0:T(8,128)(2,1)S(1)} %get-tuple-element.33.refs_0_), channel_id=1, source_target_pairs={{0,16},{8,24},{16,0},{24,8},{1,17},{9,25},{17,1},{25,9},{2,18},{10... | collective-permute-start | bytes 1081352 | tf_op jit(solution)/shard_map/ppermute | solution.py:40
  143.6 15.7 %collective-permute-start.20 = (bf16[128,1408]{1,0:T(8,128)(2,1)S(1)}, bf16[128,1408]{1,0:T(8,128)(2,1)S(1)}, u32[]{:S(2)}, u32[]{:S(2)}) collective-permute-start(bf16[128,1408]{1,0:T(8,128)(2,1)S(1)} %get-tuple-element.33.refs_0_), channel_id=1, source_target_pairs={{0,24},{8,0},{16,8},{24,16},{1,25},{9,1},{17,9},{25,17},{2,26},{10... | collective-permute-start | bytes 1081352 | tf_op jit(solution)/shard_map/ppermute | solution.py:40
  163.0 29.4 %copy-start.9 = (bf16[256,256]{1,0:T(8,128)(2,1)S(1)}, bf16[256,256]{1,0:T(8,128)(2,1)}, u32[]{:S(2)}) copy-start(bf16[256,256]{1,0:T(8,128)(2,1)} %copy-done.7) | copy-start | bytes 393220
  163.0 38.7 %copy-start.2 = (bf16[1,256,1024]{2,1,0:T(8,128)(2,1)S(1)}, bf16[1,256,1024]{2,1,0:T(8,128)(2,1)}, u32[]{:S(2)}) copy-start(bf16[1,256,1024]{2,1,0:T(8,128)(2,1)} %param.9) | copy-start | bytes 1572868
  195.2 78.1 %copy-start.4 = (bf16[1,128,1024]{2,1,0:T(8,128)(2,1)S(1)}, bf16[1,128,1024]{2,1,0:T(8,128)(2,1)}, u32[]{:S(2)}) copy-start(bf16[1,128,1024]{2,1,0:T(8,128)(2,1)} %param.8) | copy-start | bytes 786436
  195.2 22.3 %all-to-all-start.3 = ((bf16[32,64,256]{2,1,0:T(8,128)(2,1)}), bf16[32,64,256]{2,1,0:T(8,128)(2,1)}, u32[]{:S(2)}, u32[]{:S(2)}) async-start(bf16[32,64,256]{2,1,0:T(8,128)(2,1)} %bitcast.16), calls=%async_computation.3 | async-start | bytes 2097152 | tf_op jit(solution)/shard_map/all_to_all | solution.py:28
  201.7 40.7 %collective-permute-start.25 = (bf16[256,1024]{1,0:T(8,128)(2,1)S(1)}, bf16[256,1024]{1,0:T(8,128)(2,1)S(1)}, u32[]{:S(2)}, u32[]{:S(2)}) collective-permute-start(bf16[256,1024]{1,0:T(8,128)(2,1)S(1)} %bitcast.31), channel_id=1, source_target_pairs={{0,8},{8,16},{16,24},{24,0},{1,9},{9,17},{17,25},{25,1},{2,10},{10... | collective-permute-start | bytes 1572872 | tf_op jit(solution)/shard_map/ppermute | solution.py:40
  218.9 8.8 %collective-permute-start.21 = (bf16[64,256]{1,0:T(8,128)(2,1)S(1)}, bf16[64,256]{1,0:T(8,128)(2,1)S(1)}, u32[]{:S(2)}, u32[]{:S(2)}) collective-permute-start(bf16[64,256]{1,0:T(8,128)(2,1)S(1)} %reduce_sum.25), channel_id=1, source_target_pairs={{0,224},{32,0},{64,32},{96,64},{128,96},{160,128},{192,160},{224,1... | collective-permute-start | bytes 98312 | tf_op jit(solution)/shard_map/ppermute | solution.py:36
  228.4 28.1 %all-to-all-start.4 = ((bf16[8,64,256]{2,1,0:T(8,128)(2,1)}), bf16[8,64,256]{2,1,0:T(8,128)(2,1)S(1)}, u32[]{:S(2)}, u32[]{:S(2)}) async-start(bf16[8,64,256]{2,1,0:T(8,128)(2,1)} %broadcast_in_dim.26), calls=%async_computation.4 | async-start | bytes 524288 | tf_op jit(solution)/shard_map/all_to_all | solution.py:28
  231.9 41.5 %collective-permute-start.26 = (bf16[256,1024]{1,0:T(8,128)(2,1)S(1)}, bf16[256,1024]{1,0:T(8,128)(2,1)}, u32[]{:S(2)}, u32[]{:S(2)}) collective-permute-start(bf16[256,1024]{1,0:T(8,128)(2,1)S(1)} %bitcast.32), channel_id=1, source_target_pairs={{0,16},{8,24},{16,0},{24,8},{1,17},{9,25},{17,1},{25,9},{2,18},{10... | collective-permute-start | bytes 1572872 | tf_op jit(solution)/shard_map/ppermute | solution.py:40
  232.0 41.4 %collective-permute-start.27 = (bf16[256,1024]{1,0:T(8,128)(2,1)S(1)}, bf16[256,1024]{1,0:T(8,128)(2,1)}, u32[]{:S(2)}, u32[]{:S(2)}) collective-permute-start(bf16[256,1024]{1,0:T(8,128)(2,1)S(1)} %bitcast.33), channel_id=1, source_target_pairs={{0,24},{8,0},{16,8},{24,16},{1,25},{9,1},{17,9},{25,17},{2,26},{10... | collective-permute-start | bytes 1572872 | tf_op jit(solution)/shard_map/ppermute | solution.py:40
  232.7 0.9 copy-start.12
  235.3 8.8 %collective-permute-start.28 = (bf16[256,256]{1,0:T(8,128)(2,1)S(1)}, bf16[256,256]{1,0:T(8,128)(2,1)S(1)}, u32[]{:S(2)}, u32[]{:S(2)}) collective-permute-start(bf16[256,256]{1,0:T(8,128)(2,1)S(1)} %get-tuple-element.40), channel_id=1, source_target_pairs={{0,0},{1,1},{8,2},{9,3},{16,4},{17,5},{24,6},{25,7},{2,8},{3,9},{1... | collective-permute-start | bytes 393224 | tf_op jit(solution)/shard_map/ppermute | solution.py:418
  236.0 20.6 %collective-permute-start.29 = (bf16[256,256]{1,0:T(8,128)(2,1)}, bf16[256,256]{1,0:T(8,128)(2,1)S(1)}, u32[]{:S(2)}, u32[]{:S(2)}) collective-permute-start(bf16[256,256]{1,0:T(8,128)(2,1)} %get-tuple-element.41), channel_id=1, source_target_pairs={{2,0},{3,1},{10,2},{11,3},{18,4},{19,5},{26,6},{27,7},{4,8},{5,9},... | collective-permute-start | bytes 393224 | tf_op jit(solution)/shard_map/ppermute | solution.py:418
  242.4 15.7 %collective-permute-start.30 = (bf16[256,256]{1,0:T(8,128)(2,1)}, bf16[256,256]{1,0:T(8,128)(2,1)S(1)}, u32[]{:S(2)}, u32[]{:S(2)}) collective-permute-start(bf16[256,256]{1,0:T(8,128)(2,1)} %get-tuple-element.42), channel_id=1, source_target_pairs={{4,0},{5,1},{12,2},{13,3},{20,4},{21,5},{28,6},{29,7},{6,8},{7,9},... | collective-permute-start | bytes 393224 | tf_op jit(solution)/shard_map/ppermute | solution.py:418
  244.1 20.7 %collective-permute-start.31 = (bf16[256,256]{1,0:T(8,128)(2,1)S(1)}, bf16[256,256]{1,0:T(8,128)(2,1)S(1)}, u32[]{:S(2)}, u32[]{:S(2)}) collective-permute-start(bf16[256,256]{1,0:T(8,128)(2,1)S(1)} %get-tuple-element.43), channel_id=1, source_target_pairs={{6,0},{7,1},{14,2},{15,3},{22,4},{23,5},{30,6},{31,7},{0,8},{1,9},... | collective-permute-start | bytes 393224 | tf_op jit(solution)/shard_map/ppermute | solution.py:418
  256.6 19.7 %collective-permute-start.22 = (bf16[128,256]{1,0:T(8,128)(2,1)S(1)}, bf16[128,256]{1,0:T(8,128)(2,1)S(1)}, u32[]{:S(2)}, u32[]{:S(2)}) collective-permute-start(bf16[128,256]{1,0:T(8,128)(2,1)S(1)} %get-tuple-element.50), channel_id=1, source_target_pairs={{0,8},{8,16},{16,24},{24,0},{1,9},{9,17},{17,25},{25,1},{2,10},{10... | collective-permute-start | bytes 196616 | tf_op jit(solution)/shard_map/ppermute | solution.py:40
  258.1 18.2 %collective-permute-start.23 = (bf16[128,256]{1,0:T(8,128)(2,1)S(1)}, bf16[128,256]{1,0:T(8,128)(2,1)S(1)}, u32[]{:S(2)}, u32[]{:S(2)}) collective-permute-start(bf16[128,256]{1,0:T(8,128)(2,1)S(1)} %get-tuple-element.49), channel_id=1, source_target_pairs={{0,16},{8,24},{16,0},{24,8},{1,17},{9,25},{17,1},{25,9},{2,18},{10... | collective-permute-start | bytes 196616 | tf_op jit(solution)/shard_map/ppermute | solution.py:40
  264.8 11.5 %collective-permute-start.24 = (bf16[128,256]{1,0:T(8,128)(2,1)S(1)}, bf16[128,256]{1,0:T(8,128)(2,1)S(1)}, u32[]{:S(2)}, u32[]{:S(2)}) collective-permute-start(bf16[128,256]{1,0:T(8,128)(2,1)S(1)} %get-tuple-element.48), channel_id=1, source_target_pairs={{0,24},{8,0},{16,8},{24,16},{1,25},{9,1},{17,9},{25,17},{2,26},{10... | collective-permute-start | bytes 196616 | tf_op jit(solution)/shard_map/ppermute | solution.py:40
  (2 other events, 1.4 us)
